TPU v7x, 32 devices: a whole 2x2x4 slice. The times are simulated.
32 devices in a mesh: row: 16 (over z, x, core), col: 2 (over y).
Axes of the slice: x: 2, y: 2, z: 4, core: 2. Of those that a mesh axis runs over, the one named last changes fastest.
Arguments:
- g_occupied: bfloat16 [64, 512, 512], P(('row', 'col')), may hold values from -6 to 6
- g_virtual: bfloat16 [64, 512, 512], P(('row', 'col')), may hold values from -6 to 6
- owner: int32 [64, 1], P(('row', 'col')), may hold values from 0 to 1; in each aligned block of 2 rows (0 to 1, 2 to 3, ...) at most 2 rows name the same one
- coulomb: bfloat16 [1024, 3072], P('col', 'row'), may hold values from -0.25 to 0.25
Outputs:
- screened: bfloat16 [16384, 3072], P(('row', 'col'))
Inputs may be any that keep to these rules, and one draw needn't show every extreme that they name: `owner`: among the 2 pairs of one device, no tile column is named more than twice, and some device names one twice.
All inputs are finite; a program needn't handle non-finite values.
Results may differ from a plain program's by a relative error of at most 0.015.
Values may be sent and summed in bfloat16 or wider, within the bound.
No kernel may reach another device: no remote copies, remote signals or barrier semaphores. Data moves between devices by JAX's collectives and lax.ppermute only.
A program may use at most 64 MiB of HBM per device.

v0:
```python
import jax
import jax.numpy as jnp
from jax import lax
from jax.sharding import PartitionSpec as P


def body(g_occupied, g_virtual, owner, coulomb):
    n_col = lax.axis_size("col")
    pol = g_occupied.astype(jnp.float32) * g_virtual.astype(jnp.float32)
    targets = owner[:, 0]
    columns = jnp.arange(n_col, dtype=jnp.int32)
    onehot = (targets[:, None] == columns[None, :]).astype(jnp.float32)
    contrib = jnp.einsum("sd,sij->dij", onehot, pol).astype(jnp.bfloat16)
    received = lax.all_to_all(contrib, "col", split_axis=0, concat_axis=0, tiled=True)
    tile = jnp.sum(received.astype(jnp.float32), axis=0).astype(jnp.bfloat16)
    result = jnp.dot(
        tile, lax.all_gather(coulomb, "row", axis=1, tiled=True), preferred_element_type=jnp.float32
    )
    return result.astype(jnp.bfloat16)


def solution(mesh):
    return jax.shard_map(
        body,
        mesh=mesh,
        in_specs=(
            P(("row", "col"), None, None),
            P(("row", "col"), None, None),
            P(("row", "col"), None),
            P("col", "row"),
        ),
        out_specs=P(("row", "col"), None),
        check_vma=False,
    )
```

profile of v0, /device:TPU:0, one launch (start us, length us, event | category | flops | bytes accessed | tf_op | source)
XLA Modules:
  0.0 70.0 jit_solution(15090743242697294910)
XLA Ops:
  6.5 0.0 copy-start
  6.5 0.0 all-gather.2.cloned.1.call-start
  6.5 0.7 %all-gather.2.cloned.1.call-update = ((bf16[512,192]{0,1:T(8,128)(2,1)}), bf16[512,3072]{0,1:T(8,128)(2,1)}) async-update(((), (), s32[]{:S(2)}) %all-gather.2.cloned.1.call-start, bf16[512,192]{0,1:T(8,128)(2,1)} %param.7) | async-update | bytes 3538968
  7.3 1.8 %convert_multiply_fusion = bf16[2,512,512]{2,1,0:T(8,128)(2,1)S(1)} fusion(bf16[2,512,512]{2,1,0:T(8,128)(2,1)} %param.5, bf16[2,512,512]{2,1,0:T(8,128)(2,1)} %param.4), kind=kLoop, calls=%fused_computation.2 | loop fusion | flops 2097152 | bytes 3145728 | tf_op jit(solution)/shard_map/mul | solution.py:9
  9.1 0.0 copy-done
  9.1 1.9 %fusion = bf16[2,512,512]{2,0,1:T(2,128)(2,1)S(1)} fusion(bf16[2,512,512]{2,1,0:T(8,128)(2,1)S(1)} %convert_multiply_fusion, s32[2]{0:T(128)S(1)} %bitcast.6), kind=kOutput, calls=%fused_computation.3 | convolution fusion | flops 2097156 | bytes 2097160 | tf_op jit(solution)/shard_map/sd,sij->dij/dot_general | solution.py:13
  11.0 0.2 copy.10
  11.2 17.6 %all_to_all.5 = bf16[2,512,512]{2,1,0:T(8,128)(2,1)S(1)} all-to-all(bf16[2,512,512]{2,1,0:T(8,128)(2,1)S(1)} %copy.10), channel_id=1, replica_groups=mesh['row'=16,'col'=2] {'col'}, dimensions={0} | all-to-all | bytes 2097152 | tf_op jit(solution)/shard_map/all_to_all | solution.py:14
  28.8 0.5 reduce_sum.12
  29.3 28.5 %all-gather.2.cloned.1.call-done = bf16[512,3072]{0,1:T(8,128)(2,1)} async-done(((bf16[512,192]{0,1:T(8,128)(2,1)}), bf16[512,3072]{0,1:T(8,128)(2,1)}) %all-gather.2.cloned.1.call-update) | async-done | bytes 3145744 | tf_op jit(solution)/shard_map/all_gather | solution.py:17
  57.8 5.4 %convolution_convert_fusion = bf16[512,3072]{1,0:T(8,128)(2,1)} fusion(bf16[512,512]{1,0:T(8,128)(2,1)S(1)} %reduce_sum.12, bf16[512,3072]{0,1:T(8,128)(2,1)} %all-gather.2.cloned.1.call-done), kind=kOutput, calls=%fused_computation | convolution fusion | flops 1612185600 | bytes 6815744 | tf_op jit(solution)/shard_map/dot_general | solution.py:16
Async XLA Ops:
  6.5 2.6 %copy-start = (s32[2,1]{0,1:T(1,128)S(1)}, s32[2,1]{0,1:T(1,128)}, u32[]{:S(2)}) copy-start(s32[2,1]{0,1:T(1,128)} %param.6) | copy-start | bytes 28
  6.5 51.2 %all-gather.2.cloned.1.call-start = ((), (), s32[]{:S(2)}) async-start(), calls=%async_computation.1 | async-start | bytes 3342336 | tf_op jit(solution)/shard_map/all_gather | solution.py:17
Sparse Core Ops, SparseCore 0:
  9.6 48.0 all-gather.1
where the time goes:
time: 70.2 us; the launch traced here: 70 us
  waiting for transfers between devices  29.2 us (42%)
  blocking collectives  17.6 us (25%)
  between operations  13.4 us (19%)
  matrix products  7.25 us (10%)
  other arithmetic  2.32 us (3%)
    all_gather x1, waiting for transfers between devices, body(): lax.all_gather(coulomb, 'row', axis=1, tiled=True)  28.5 us
    all_to_all x1, blocking collectives, body(): lax.all_to_all(contrib, 'col', split_axis=0, concat_axis=0, tiled=True)  17.6 us
    dot_general x1, matrix products, body(): jnp.dot(tile, lax.all_gather(coulomb, 'row', axis=1, tiled=True), preferr...  5.38 us
    dot_general x1, matrix products, body(): contrib = jnp.einsum('sd,sij->dij', onehot, pol).astype(jnp.bfloat16)  1.87 us
    mul x1, other arithmetic, body(): pol = g_occupied.astype(jnp.float32) * g_virtual.astype(jnp.float32)  1.83 us
  transfers between devices with their start and end apart: 1, of which 1 were waited for; matrix products, arithmetic and copies ran while one was open for 6% of the time, Pallas kernels for 0%

commit v1 on v0

v1 whole, which is shorter than its diff:
```python
import functools
import math

import jax
import jax.numpy as jnp
import numpy as np
from jax import lax
from jax.experimental import pallas as pl
from jax.experimental.pallas import tpu as pltpu
from jax.sharding import PartitionSpec as P

AXES = ("row", "col")


def chip_ring(mesh):
    n_row, n_col = mesh.devices.shape
    row_of = {}
    for r in range(n_row):
        for c in range(n_col):
            d = mesh.devices[r, c]
            row_of[(*d.coords, d.core_on_chip)] = (r, c)
    chips = sorted({k[:3] for k, (_, c) in row_of.items() if c == 0})
    if len(chips) * 2 != n_row:
        return None
    spans = [sorted({k[a] for k in chips}) for a in range(3)]
    wide = [a for a in range(3) if len(spans[a]) > 1]
    if len(wide) != 2 or math.prod(len(s) for s in spans) != len(chips):
        return None
    short, long = sorted(wide, key=lambda a: len(spans[a]))
    if len(spans[short]) != 2:
        return None
    lo, hi = spans[short]
    order = [(lo, v) for v in spans[long]] + [(hi, v) for v in reversed(spans[long])]
    place = {sv: i for i, sv in enumerate(order)}
    n = len(order)
    position = np.zeros((n_row, n_col), np.int32)
    core = np.zeros((n_row, n_col), np.int32)
    flat = {}
    for k, (r, c) in row_of.items():
        position[r, c] = place[(k[short], k[long])]
        core[r, c] = k[3]
        flat[(position[r, c], core[r, c], c)] = r * n_col + c
    slot = np.zeros((n_col, n), np.int32)
    for (p, k, c), f in flat.items():
        r = f // n_col
        if r % 2 != k:
            return None
        slot[c, p] = r // 2
    if (slot != slot[:1]).any():
        return None
    return n, position, core, flat, slot[0]


def matmul_kernel(n_chips, slots_ref, own_ref, recv_ref, *refs):
    pieces = refs[: 2 * n_chips]
    out_ref, panel, own, recv, tile, block, piece_sem, tile_sem, out_sem = refs[2 * n_chips :]
    width = 2 * panel.shape[2]
    cols = slots_ref.shape[0] // n_chips
    device = lax.axis_index("row")
    core = lax.rem(device, 2)
    base = device * n_chips

    def fetch(j, k):
        return pltpu.make_async_copy(pieces[2 * j + k], panel.at[j, k ^ core], piece_sem.at[j, k])

    def put(j):
        at = pl.multiple_of(slots_ref[base + j] * width, width)
        return pltpu.make_async_copy(block.at[j % 2], out_ref.at[:, pl.ds(at, width)], out_sem.at[j % 2])

    own_copy = pltpu.make_async_copy(own_ref, own, tile_sem.at[0])
    recv_copy = pltpu.make_async_copy(recv_ref, recv, tile_sem.at[1])
    own_copy.start()
    recv_copy.start()
    for j in range(n_chips):
        fetch(j, 0).start()
        fetch(j, 1).start()
    own_copy.wait()
    recv_copy.wait()
    tile[...] = (own[...].astype(jnp.float32) + recv[...].astype(jnp.float32)).astype(tile.dtype)
    for j in range(n_chips):
        fetch(j, 0).wait()
        fetch(j, 1).wait()
        if j >= 2:
            put(j - 2).wait()
        pair = panel[j].reshape(width, panel.shape[3])
        block[j % 2] = lax.dot_general(
            tile[...], pair, (((1,), (1,)), ((), ())), preferred_element_type=jnp.float32
        ).astype(block.dtype)
        put(j).start()
    put(n_chips - 2).wait()
    put(n_chips - 1).wait()


def ring_body(ring, g_occupied, g_virtual, owner, coulomb):
    n_chips, position, core, flat, slot = ring
    n_row, n_col = position.shape
    half = n_chips // 2

    def pairs(step):
        out = []
        for r in range(n_row):
            for c in range(n_col):
                p, k = step(int(position[r, c]), int(core[r, c]))
                out.append((r * n_col + c, flat[(p % n_chips, k, c)]))
        return out

    onward = pairs(lambda p, k: (p + 1 - 2 * k, k))
    across = pairs(lambda p, k: (p, 1 - k))

    me = lax.axis_index("col")
    pol = g_occupied.astype(jnp.float32) * g_virtual.astype(jnp.float32)

    def contribution(d):
        return jnp.sum(jnp.where(owner[:, :, None] == d, pol, 0.0), axis=0).astype(jnp.bfloat16)

    other = contribution(1 - me)
    own = contribution(me)
    received = lax.ppermute(other, "col", [(0, 1), (1, 0)])

    mine = coulomb.T
    sibling = lax.ppermute(mine, AXES, across)
    first, second = [mine], [sibling]
    for i in range(half):
        first.append(lax.ppermute(first[-1], AXES, onward))
        if i + 1 < half:
            second.append(lax.ppermute(second[-1], AXES, onward))
    pieces = [mine, sibling]
    for i in range(1, half + 1):
        a = lax.ppermute(first[i], AXES, across)
        if i < half:
            b = lax.ppermute(second[i], AXES, across)
            pieces += [first[i], second[i], b, a]
        else:
            pieces += [first[i], a]

    table = np.zeros((n_row, n_chips), np.int32)
    for r in range(n_row):
        p, way = int(position[r, 0]), 1 - 2 * int(core[r, 0])
        order = [p]
        for i in range(1, half + 1):
            order += [p - way * i, p + way * i] if i < half else [p - way * i]
        table[r] = [slot[q % n_chips] for q in order]

    width, depth = mine.shape
    rows = own.shape[0]
    any_spec = pl.BlockSpec(memory_space=pl.ANY)
    return pl.pallas_call(
        functools.partial(matmul_kernel, n_chips),
        out_shape=jax.ShapeDtypeStruct((rows, 2 * n_chips * width), jnp.bfloat16),
        in_specs=[pl.BlockSpec(memory_space=pltpu.SMEM)] + [any_spec] * (2 + 2 * n_chips),
        out_specs=any_spec,
        scratch_shapes=[
            pltpu.VMEM((n_chips, 2, width, depth), jnp.bfloat16),
            pltpu.VMEM((rows, depth), jnp.bfloat16),
            pltpu.VMEM((rows, depth), jnp.bfloat16),
            pltpu.VMEM((rows, depth), jnp.bfloat16),
            pltpu.VMEM((2, rows, 2 * width), jnp.bfloat16),
            pltpu.SemaphoreType.DMA((n_chips, 2)),
            pltpu.SemaphoreType.DMA((2,)),
            pltpu.SemaphoreType.DMA((2,)),
        ],
        compiler_params=pltpu.CompilerParams(vmem_limit_bytes=16 << 20),
        cost_estimate=pl.CostEstimate(
            flops=2 * rows * depth * 2 * n_chips * width,
            bytes_accessed=2 * n_chips * width * (rows + depth) * 2,
            transcendentals=0,
        ),
    )(jnp.asarray(table.reshape(-1)), own, received, *pieces)


def gather_body(g_occupied, g_virtual, owner, coulomb):
    n_col = lax.axis_size("col")
    pol = g_occupied.astype(jnp.float32) * g_virtual.astype(jnp.float32)
    columns = jnp.arange(n_col, dtype=jnp.int32)
    onehot = (owner[:, 0][:, None] == columns[None, :]).astype(jnp.float32)
    contrib = jnp.einsum("sd,sij->dij", onehot, pol).astype(jnp.bfloat16)
    received = lax.all_to_all(contrib, "col", split_axis=0, concat_axis=0, tiled=True)
    tile = jnp.sum(received.astype(jnp.float32), axis=0).astype(jnp.bfloat16)
    panel = lax.all_gather(coulomb, "row", axis=1, tiled=True)
    return jnp.dot(tile, panel, preferred_element_type=jnp.float32).astype(jnp.bfloat16)


def solution(mesh):
    ring = chip_ring(mesh) if mesh.shape["col"] == 2 else None
    return jax.shard_map(
        functools.partial(ring_body, ring) if ring else gather_body,
        mesh=mesh,
        in_specs=(P(AXES, None, None), P(AXES, None, None), P(AXES, None), P("col", "row")),
        out_specs=P(AXES, None),
        check_vma=False,
    )
```

time: 70.2 us -> 39.7 us (0.57)
  waiting for transfers between devices: 29.2 us -> 10.8 us
  blocking collectives: 17.6 us -> 0 us
  starting transfers between devices: 0.01 us -> 15.5 us
  between operations: 13.4 us -> 0.05 us
  Pallas kernels: 0 us -> 10.4 us
  matrix products: 7.25 us -> 0 us
    all_gather x1 -> x0, waiting for transfers between devices: 28.5 us -> none  [body(): lax.all_gather(coulomb, 'row', axis=1, tiled=True)]
    all_to_all x1 -> x0, blocking collectives: 17.6 us -> none  [body(): lax.all_to_all(contrib, 'col', split_axis=0, concat_axis=0, tiled=True)]
    ppermute x0 -> x16, starting transfers between devices: none -> 15.5 us  [the longest x4 8.25 us: ring_body(): first.append(lax.ppermute(first[-1], AXES, onward))]
    ppermute x0 -> x16, waiting for transfers between devices: none -> 10.8 us  [the longest x4 5.41 us: ring_body(): first.append(lax.ppermute(first[-1], AXES, onward))]
    pallas_call x0 -> x1, Pallas kernels: none -> 10.4 us  [ring_body(): pl.pallas_call(functools.partial(matmul_kernel, n_chips), out_shape=jax.S...]
    dot_general x2 -> x0, matrix products: 7.25 us -> none  [the longest x1 5.38 us: body(): jnp.dot(tile, lax.all_gather(coulomb, 'row', axis=1, tiled=True), preferr...]
    mul x1 -> x0, other arithmetic: 1.83 us -> none  [body(): pol = g_occupied.astype(jnp.float32) * g_virtual.astype(jnp.float32)]
    reduce_sum x1, other arithmetic: 0.49 us -> 2.15 us  [contribution(): jnp.sum(jnp.where(owner[:, :, None] == d, pol, 0.0), axis=0)]
  transfers between devices with their start and end apart: 1 -> 16, of which waited for: 1 -> 7; matrix products, arithmetic and copies ran while one was open for 6% -> 7% of each run, Pallas kernels for 0% -> 0%
where the time goes in v1:
time: 39.7 us; the launch traced here: 39.5 us
  starting transfers between devices  15.5 us (39%)
  waiting for transfers between devices  10.8 us (27%)
  Pallas kernels  10.4 us (26%)
  other arithmetic  2.81 us (7%)
    pallas_call x1, Pallas kernels, ring_body(): pl.pallas_call(functools.partial(matmul_kernel, n_chips), out_shape=jax.S...  10.4 us
    ppermute x4, starting transfers between devices, ring_body(): first.append(lax.ppermute(first[-1], AXES, onward))  8.25 us
    ppermute x4, waiting for transfers between devices, ring_body(): first.append(lax.ppermute(first[-1], AXES, onward))  5.41 us
    ppermute x3, starting transfers between devices, ring_body(): second.append(lax.ppermute(second[-1], AXES, onward))  4.65 us
    ppermute x3, waiting for transfers between devices, ring_body(): second.append(lax.ppermute(second[-1], AXES, onward))  2.64 us
    reduce_sum x1, other arithmetic, contribution(): jnp.sum(jnp.where(owner[:, :, None] == d, pol, 0.0), axis=0)  2.15 us
    ppermute x1, starting transfers between devices, ring_body(): received = lax.ppermute(other, 'col', [(0, 1), (1, 0)])  1.58 us
    ppermute x3, waiting for transfers between devices, ring_body(): b = lax.ppermute(second[i], AXES, across)  1.41 us
  transfers between devices with their start and end apart: 16, of which 7 were waited for; matrix products, arithmetic and copies ran while one was open for 7% of the time, Pallas kernels for 0%

profile of v1, /device:TPU:0, one launch (start us, length us, event | category | flops | bytes accessed | tf_op | source)
XLA Modules:
  0.0 39.5 jit_solution(12467450359244167408)
XLA Ops:
  0.0 3.0 %collective-permute-start.2 = (bf16[192,512]{1,0:T(8,128)(2,1)}, bf16[192,512]{1,0:T(8,128)(2,1)S(1)}, u32[]{:S(2)}, u32[]{:S(2)}) collective-permute-start(bf16[192,512]{1,0:T(8,128)(2,1)} %bitcast.5), channel_id=1, source_target_pairs={{0,8},{1,9},{2,6},{3,7},{4,0},{5,1},{6,14},{7,15},{8,16},{9,17},{1... | collective-permute-start | bytes 589832 | tf_op jit(solution)/shard_map/ppermute | solution.py:124
  3.0 0.7 %compare_bitcast_fusion.1 = (pred[2]{0:T(512)(128)(4,1)S(1)}, pred[2]{0:T(512)(128)(4,1)S(1)}) fusion(s32[2,1]{0,1:T(1,128)} %param.7, s32[]{:T(128)S(6)} %axis_index.12, s32[]{:T(128)S(6)} %sub.3), kind=kLoop, calls=%fused_computation.4 | loop fusion | flops 4 | bytes 20 | tf_op jit(solution)/shard_map/eq | solution.py:114
  3.7 3.1 %collective-permute-done.2.refs_2_ = bf16[192,512]{1,0:T(8,128)(2,1)S(1)} collective-permute-done((bf16[192,512]{1,0:T(8,128)(2,1)}, bf16[192,512]{1,0:T(8,128)(2,1)S(1)}, u32[]{:S(2)}, u32[]{:S(2)}) %collective-permute-start.2) | collective-permute-done | bytes 196640 | tf_op jit(solution)/shard_map/ppermute | solution.py:124
  6.8 2.1 %collective-permute-start.6 = (bf16[192,512]{1,0:T(8,128)(2,1)S(1)}, bf16[192,512]{1,0:T(8,128)(2,1)S(1)}, u32[]{:S(2)}, u32[]{:S(2)}) collective-permute-start(bf16[192,512]{1,0:T(8,128)(2,1)S(1)} %collective-permute-done.2.refs_2_), channel_id=1, source_target_pairs={{0,8},{1,9},{2,6},{3,7},{4,0},{5,1},{6,14},{7,15},{8,16},{9,17},{1... | collective-permute-start | bytes 589832 | tf_op jit(solution)/shard_map/ppermute | solution.py:124
  8.9 0.0 collective-permute-done.1.refs_1_
  8.9 1.6 %collective-permute-start.3 = (bf16[192,512]{1,0:T(8,128)(2,1)S(1)}, bf16[192,512]{1,0:T(8,128)(2,1)S(1)}, u32[]{:S(2)}, u32[]{:S(2)}) collective-permute-start(bf16[192,512]{1,0:T(8,128)(2,1)S(1)} %collective-permute-done.1.refs_1_), channel_id=1, source_target_pairs={{0,8},{1,9},{2,6},{3,7},{4,0},{5,1},{6,14},{7,15},{8,16},{9,17},{1... | collective-permute-start | bytes 589832 | tf_op jit(solution)/shard_map/ppermute | solution.py:126
  10.5 2.1 %select_reduce_fusion = (bf16[512,512]{1,0:T(8,128)(2,1)S(1)}, bf16[512,512]{1,0:T(8,128)(2,1)S(1)}) fusion(bf16[2,512,512]{2,1,0:T(8,128)(2,1)} %param.6, bf16[2,512,512]{2,1,0:T(8,128)(2,1)} %param.5, pred[2]{0:T(512)(128)(4,1)S(1)} %get-tuple-element.8, pred[2]{0:T(512)(128)(4,1)S(1)} %get-tuple-element.7), kind=kLoop, calls=%fused_computation | loop fusion | flops 3145728 | bytes 3145732 | tf_op jit(solution)/shard_map/reduce_sum | solution.py:114
  12.6 1.6 %collective-permute-start = (bf16[512,512]{1,0:T(8,128)(2,1)S(1)}, bf16[512,512]{1,0:T(8,128)(2,1)S(1)}, u32[]{:S(2)}, u32[]{:S(2)}) collective-permute-start(bf16[512,512]{1,0:T(8,128)(2,1)S(1)} %get-tuple-element.5), channel_id=1, source_target_pairs={{0,1},{1,0},{2,3},{3,2},{4,5},{5,4},{6,7},{7,6},{8,9},{9,8},{10,11... | collective-permute-start | bytes 1572872 | tf_op jit(solution)/shard_map/ppermute | solution.py:118
  14.2 0.0 collective-permute-done.6.refs_6_
  14.2 1.6 %collective-permute-start.10 = (bf16[192,512]{1,0:T(8,128)(2,1)S(1)}, bf16[192,512]{1,0:T(8,128)(2,1)S(1)}, u32[]{:S(2)}, u32[]{:S(2)}) collective-permute-start(bf16[192,512]{1,0:T(8,128)(2,1)S(1)} %collective-permute-done.6.refs_6_), channel_id=1, source_target_pairs={{0,8},{1,9},{2,6},{3,7},{4,0},{5,1},{6,14},{7,15},{8,16},{9,17},{1... | collective-permute-start | bytes 589832 | tf_op jit(solution)/shard_map/ppermute | solution.py:124
  15.8 0.0 collective-permute-done.3.refs_3_
  15.8 1.5 %collective-permute-start.7 = (bf16[192,512]{1,0:T(8,128)(2,1)S(1)}, bf16[192,512]{1,0:T(8,128)(2,1)S(1)}, u32[]{:S(2)}, u32[]{:S(2)}) collective-permute-start(bf16[192,512]{1,0:T(8,128)(2,1)S(1)} %collective-permute-done.3.refs_3_), channel_id=1, source_target_pairs={{0,8},{1,9},{2,6},{3,7},{4,0},{5,1},{6,14},{7,15},{8,16},{9,17},{1... | collective-permute-start | bytes 589832 | tf_op jit(solution)/shard_map/ppermute | solution.py:126
  17.3 0.5 %collective-permute-start.9 = (bf16[192,512]{1,0:T(8,128)(2,1)S(1)}, bf16[192,512]{1,0:T(8,128)(2,1)S(1)}, u32[]{:S(2)}, u32[]{:S(2)}) collective-permute-start(bf16[192,512]{1,0:T(8,128)(2,1)S(1)} %collective-permute-done.6.refs_6_), channel_id=1, source_target_pairs={{0,2},{1,3},{2,0},{3,1},{4,6},{5,7},{6,4},{7,5},{8,10},{9,11},{10,... | collective-permute-start | bytes 589832 | tf_op jit(solution)/shard_map/ppermute | solution.py:129
  17.8 2.1 %collective-permute-done.10.refs_10_ = bf16[192,512]{1,0:T(8,128)(2,1)S(1)} collective-permute-done((bf16[192,512]{1,0:T(8,128)(2,1)S(1)}, bf16[192,512]{1,0:T(8,128)(2,1)S(1)}, u32[]{:S(2)}, u32[]{:S(2)}) %collective-permute-start.10) | collective-permute-done | bytes 196640 | tf_op jit(solution)/shard_map/ppermute | solution.py:124
  19.9 1.6 %collective-permute-start.14 = (bf16[192,512]{1,0:T(8,128)(2,1)S(1)}, bf16[192,512]{1,0:T(8,128)(2,1)S(1)}, u32[]{:S(2)}, u32[]{:S(2)}) collective-permute-start(bf16[192,512]{1,0:T(8,128)(2,1)S(1)} %collective-permute-done.10.refs_10_), channel_id=1, source_target_pairs={{0,8},{1,9},{2,6},{3,7},{4,0},{5,1},{6,14},{7,15},{8,16},{9,17},{1... | collective-permute-start | bytes 589832 | tf_op jit(solution)/shard_map/ppermute | solution.py:124
  21.5 0.5 %collective-permute-done.7.refs_7_ = bf16[192,512]{1,0:T(8,128)(2,1)S(1)} collective-permute-done((bf16[192,512]{1,0:T(8,128)(2,1)S(1)}, bf16[192,512]{1,0:T(8,128)(2,1)S(1)}, u32[]{:S(2)}, u32[]{:S(2)}) %collective-permute-start.7) | collective-permute-done | bytes 196640 | tf_op jit(solution)/shard_map/ppermute | solution.py:126
  22.0 1.6 %collective-permute-start.11 = (bf16[192,512]{1,0:T(8,128)(2,1)S(1)}, bf16[192,512]{1,0:T(8,128)(2,1)S(1)}, u32[]{:S(2)}, u32[]{:S(2)}) collective-permute-start(bf16[192,512]{1,0:T(8,128)(2,1)S(1)} %collective-permute-done.7.refs_7_), channel_id=1, source_target_pairs={{0,8},{1,9},{2,6},{3,7},{4,0},{5,1},{6,14},{7,15},{8,16},{9,17},{1... | collective-permute-start | bytes 589832 | tf_op jit(solution)/shard_map/ppermute | solution.py:126
  23.6 1.3 %collective-permute-done.recv_ref = bf16[512,512]{1,0:T(8,128)(2,1)S(1)} collective-permute-done((bf16[512,512]{1,0:T(8,128)(2,1)S(1)}, bf16[512,512]{1,0:T(8,128)(2,1)S(1)}, u32[]{:S(2)}, u32[]{:S(2)}) %collective-permute-start) | collective-permute-done | bytes 524320 | tf_op jit(solution)/shard_map/ppermute | solution.py:118
  24.9 0.0 collective-permute-done.9.refs_9_
  24.9 0.5 %collective-permute-start.8 = (bf16[192,512]{1,0:T(8,128)(2,1)S(1)}, bf16[192,512]{1,0:T(8,128)(2,1)S(1)}, u32[]{:S(2)}, u32[]{:S(2)}) collective-permute-start(bf16[192,512]{1,0:T(8,128)(2,1)S(1)} %collective-permute-done.7.refs_7_), channel_id=1, source_target_pairs={{0,2},{1,3},{2,0},{3,1},{4,6},{5,7},{6,4},{7,5},{8,10},{9,11},{10,... | collective-permute-start | bytes 589832 | tf_op jit(solution)/shard_map/ppermute | solution.py:131
  25.4 0.2 collective-permute-done.14.refs_14_
  25.6 2.1 %collective-permute-done.11.refs_11_ = bf16[192,512]{1,0:T(8,128)(2,1)S(1)} collective-permute-done((bf16[192,512]{1,0:T(8,128)(2,1)S(1)}, bf16[192,512]{1,0:T(8,128)(2,1)S(1)}, u32[]{:S(2)}, u32[]{:S(2)}) %collective-permute-start.11) | collective-permute-done | bytes 196640 | tf_op jit(solution)/shard_map/ppermute | solution.py:126
  27.7 1.4 %collective-permute-done.12.refs_12_ = bf16[192,512]{1,0:T(8,128)(2,1)S(1)} collective-permute-done((bf16[192,512]{1,0:T(8,128)(2,1)S(1)}, bf16[192,512]{1,0:T(8,128)(2,1)S(1)}, u32[]{:S(2)}, u32[]{:S(2)}) %collective-permute-start.12) | collective-permute-done | bytes 196640 | tf_op jit(solution)/shard_map/ppermute | solution.py:131
  29.1 10.4 %shard_map.55 = bf16[512,3072]{1,0:T(8,128)(2,1)} custom-call(s32[128]{0:T(128)S(1)} %copy-done.1, bf16[512,512]{1,0:T(8,128)(2,1)S(1)} %get-tuple-element.6.own_ref, bf16[512,512]{1,0:T(8,128)(2,1)S(1)} %collective-permute-done.recv_ref, bf16[192,512]{1,0:T(8,128)(2,1)S(1)} %bitcast.7, bf16[192,512]{1,0:T(8,128)(2,1)S(1)} %collective-permute-done.1.refs_1_, ...), custom_call_target="tpu_custom_call" | custom-call | flops 1610612736 | bytes 6291456 | tf_op jit(solution)/shard_map/pallas_call | solution.py:147
  (15 shorter events, 0.0 us)
Async XLA Ops:
  0.0 29.1 %copy-start.1 = (s32[128]{0:T(128)S(1)}, s32[128]{0:T(128)}, u32[]{:S(2)}) copy-start(s32[128]{0:T(128)} %constant.10.clone.slots_ref) | copy-start | bytes 1540
  0.0 29.1 %copy-start = (bf16[512,192]{0,1:T(8,128)(2,1)S(1)}, bf16[512,192]{0,1:T(8,128)(2,1)}, u32[]{:S(2)}) copy-start(bf16[512,192]{0,1:T(8,128)(2,1)} %param.8) | copy-start | bytes 589828
  0.0 6.8 %collective-permute-start.2 = (bf16[192,512]{1,0:T(8,128)(2,1)}, bf16[192,512]{1,0:T(8,128)(2,1)S(1)}, u32[]{:S(2)}, u32[]{:S(2)}) collective-permute-start(bf16[192,512]{1,0:T(8,128)(2,1)} %bitcast.5), channel_id=1, source_target_pairs={{0,8},{1,9},{2,6},{3,7},{4,0},{5,1},{6,14},{7,15},{8,16},{9,17},{1... | collective-permute-start | bytes 589832 | tf_op jit(solution)/shard_map/ppermute | solution.py:124
  3.0 5.9 %collective-permute-start.1 = (bf16[192,512]{1,0:T(8,128)(2,1)}, bf16[192,512]{1,0:T(8,128)(2,1)S(1)}, u32[]{:S(2)}, u32[]{:S(2)}) collective-permute-start(bf16[192,512]{1,0:T(8,128)(2,1)} %bitcast.6), channel_id=1, source_target_pairs={{0,2},{1,3},{2,0},{3,1},{4,6},{5,7},{6,4},{7,5},{8,10},{9,11},{10,... | collective-permute-start | bytes 589832 | tf_op jit(solution)/shard_map/ppermute | solution.py:121
  6.8 7.4 %collective-permute-start.6 = (bf16[192,512]{1,0:T(8,128)(2,1)S(1)}, bf16[192,512]{1,0:T(8,128)(2,1)S(1)}, u32[]{:S(2)}, u32[]{:S(2)}) collective-permute-start(bf16[192,512]{1,0:T(8,128)(2,1)S(1)} %collective-permute-done.2.refs_2_), channel_id=1, source_target_pairs={{0,8},{1,9},{2,6},{3,7},{4,0},{5,1},{6,14},{7,15},{8,16},{9,17},{1... | collective-permute-start | bytes 589832 | tf_op jit(solution)/shard_map/ppermute | solution.py:124
  8.9 6.9 %collective-permute-start.3 = (bf16[192,512]{1,0:T(8,128)(2,1)S(1)}, bf16[192,512]{1,0:T(8,128)(2,1)S(1)}, u32[]{:S(2)}, u32[]{:S(2)}) collective-permute-start(bf16[192,512]{1,0:T(8,128)(2,1)S(1)} %collective-permute-done.1.refs_1_), channel_id=1, source_target_pairs={{0,8},{1,9},{2,6},{3,7},{4,0},{5,1},{6,14},{7,15},{8,16},{9,17},{1... | collective-permute-start | bytes 589832 | tf_op jit(solution)/shard_map/ppermute | solution.py:126
  12.6 12.2 %collective-permute-start = (bf16[512,512]{1,0:T(8,128)(2,1)S(1)}, bf16[512,512]{1,0:T(8,128)(2,1)S(1)}, u32[]{:S(2)}, u32[]{:S(2)}) collective-permute-start(bf16[512,512]{1,0:T(8,128)(2,1)S(1)} %get-tuple-element.5), channel_id=1, source_target_pairs={{0,1},{1,0},{2,3},{3,2},{4,5},{5,4},{6,7},{7,6},{8,9},{9,8},{10,11... | collective-permute-start | bytes 1572872 | tf_op jit(solution)/shard_map/ppermute | solution.py:118
  14.2 5.7 %collective-permute-start.10 = (bf16[192,512]{1,0:T(8,128)(2,1)S(1)}, bf16[192,512]{1,0:T(8,128)(2,1)S(1)}, u32[]{:S(2)}, u32[]{:S(2)}) collective-permute-start(bf16[192,512]{1,0:T(8,128)(2,1)S(1)} %collective-permute-done.6.refs_6_), channel_id=1, source_target_pairs={{0,8},{1,9},{2,6},{3,7},{4,0},{5,1},{6,14},{7,15},{8,16},{9,17},{1... | collective-permute-start | bytes 589832 | tf_op jit(solution)/shard_map/ppermute | solution.py:124
  15.8 6.2 %collective-permute-start.7 = (bf16[192,512]{1,0:T(8,128)(2,1)S(1)}, bf16[192,512]{1,0:T(8,128)(2,1)S(1)}, u32[]{:S(2)}, u32[]{:S(2)}) collective-permute-start(bf16[192,512]{1,0:T(8,128)(2,1)S(1)} %collective-permute-done.3.refs_3_), channel_id=1, source_target_pairs={{0,8},{1,9},{2,6},{3,7},{4,0},{5,1},{6,14},{7,15},{8,16},{9,17},{1... | collective-permute-start | bytes 589832 | tf_op jit(solution)/shard_map/ppermute | solution.py:126
  17.3 6.3 %collective-permute-start.5 = (bf16[192,512]{1,0:T(8,128)(2,1)S(1)}, bf16[192,512]{1,0:T(8,128)(2,1)S(1)}, u32[]{:S(2)}, u32[]{:S(2)}) collective-permute-start(bf16[192,512]{1,0:T(8,128)(2,1)S(1)} %collective-permute-done.2.refs_2_), channel_id=1, source_target_pairs={{0,2},{1,3},{2,0},{3,1},{4,6},{5,7},{6,4},{7,5},{8,10},{9,11},{10,... | collective-permute-start | bytes 589832 | tf_op jit(solution)/shard_map/ppermute | solution.py:129
  17.3 7.6 %collective-permute-start.9 = (bf16[192,512]{1,0:T(8,128)(2,1)S(1)}, bf16[192,512]{1,0:T(8,128)(2,1)S(1)}, u32[]{:S(2)}, u32[]{:S(2)}) collective-permute-start(bf16[192,512]{1,0:T(8,128)(2,1)S(1)} %collective-permute-done.6.refs_6_), channel_id=1, source_target_pairs={{0,2},{1,3},{2,0},{3,1},{4,6},{5,7},{6,4},{7,5},{8,10},{9,11},{10,... | collective-permute-start | bytes 589832 | tf_op jit(solution)/shard_map/ppermute | solution.py:129
  19.9 5.7 %collective-permute-start.14 = (bf16[192,512]{1,0:T(8,128)(2,1)S(1)}, bf16[192,512]{1,0:T(8,128)(2,1)S(1)}, u32[]{:S(2)}, u32[]{:S(2)}) collective-permute-start(bf16[192,512]{1,0:T(8,128)(2,1)S(1)} %collective-permute-done.10.refs_10_), channel_id=1, source_target_pairs={{0,8},{1,9},{2,6},{3,7},{4,0},{5,1},{6,14},{7,15},{8,16},{9,17},{1... | collective-permute-start | bytes 589832 | tf_op jit(solution)/shard_map/ppermute | solution.py:124
  22.0 5.7 %collective-permute-start.11 = (bf16[192,512]{1,0:T(8,128)(2,1)S(1)}, bf16[192,512]{1,0:T(8,128)(2,1)S(1)}, u32[]{:S(2)}, u32[]{:S(2)}) collective-permute-start(bf16[192,512]{1,0:T(8,128)(2,1)S(1)} %collective-permute-done.7.refs_7_), channel_id=1, source_target_pairs={{0,8},{1,9},{2,6},{3,7},{4,0},{5,1},{6,14},{7,15},{8,16},{9,17},{1... | collective-permute-start | bytes 589832 | tf_op jit(solution)/shard_map/ppermute | solution.py:126
  23.6 4.1 %collective-permute-start.4 = (bf16[192,512]{1,0:T(8,128)(2,1)S(1)}, bf16[192,512]{1,0:T(8,128)(2,1)S(1)}, u32[]{:S(2)}, u32[]{:S(2)}) collective-permute-start(bf16[192,512]{1,0:T(8,128)(2,1)S(1)} %collective-permute-done.3.refs_3_), channel_id=1, source_target_pairs={{0,2},{1,3},{2,0},{3,1},{4,6},{5,7},{6,4},{7,5},{8,10},{9,11},{10,... | collective-permute-start | bytes 589832 | tf_op jit(solution)/shard_map/ppermute | solution.py:131
  24.9 2.8 %collective-permute-start.13 = (bf16[192,512]{1,0:T(8,128)(2,1)S(1)}, bf16[192,512]{1,0:T(8,128)(2,1)S(1)}, u32[]{:S(2)}, u32[]{:S(2)}) collective-permute-start(bf16[192,512]{1,0:T(8,128)(2,1)S(1)} %collective-permute-done.10.refs_10_), channel_id=1, source_target_pairs={{0,2},{1,3},{2,0},{3,1},{4,6},{5,7},{6,4},{7,5},{8,10},{9,11},{10,... | collective-permute-start | bytes 589832 | tf_op jit(solution)/shard_map/ppermute | solution.py:129
  24.9 2.8 %collective-permute-start.8 = (bf16[192,512]{1,0:T(8,128)(2,1)S(1)}, bf16[192,512]{1,0:T(8,128)(2,1)S(1)}, u32[]{:S(2)}, u32[]{:S(2)}) collective-permute-start(bf16[192,512]{1,0:T(8,128)(2,1)S(1)} %collective-permute-done.7.refs_7_), channel_id=1, source_target_pairs={{0,2},{1,3},{2,0},{3,1},{4,6},{5,7},{6,4},{7,5},{8,10},{9,11},{10,... | collective-permute-start | bytes 589832 | tf_op jit(solution)/shard_map/ppermute | solution.py:131
  25.6 2.1 %collective-permute-start.15 = (bf16[192,512]{1,0:T(8,128)(2,1)S(1)}, bf16[192,512]{1,0:T(8,128)(2,1)S(1)}, u32[]{:S(2)}, u32[]{:S(2)}) collective-permute-start(bf16[192,512]{1,0:T(8,128)(2,1)S(1)} %collective-permute-done.14.refs_14_), channel_id=1, source_target_pairs={{0,2},{1,3},{2,0},{3,1},{4,6},{5,7},{6,4},{7,5},{8,10},{9,11},{10,... | collective-permute-start | bytes 589832 | tf_op jit(solution)/shard_map/ppermute | solution.py:129
  27.7 1.4 %collective-permute-start.12 = (bf16[192,512]{1,0:T(8,128)(2,1)S(1)}, bf16[192,512]{1,0:T(8,128)(2,1)S(1)}, u32[]{:S(2)}, u32[]{:S(2)}) collective-permute-start(bf16[192,512]{1,0:T(8,128)(2,1)S(1)} %collective-permute-done.11.refs_11_), channel_id=1, source_target_pairs={{0,2},{1,3},{2,0},{3,1},{4,6},{5,7},{6,4},{7,5},{8,10},{9,11},{10,... | collective-permute-start | bytes 589832 | tf_op jit(solution)/shard_map/ppermute | solution.py:131

commit v2 on v0

v2 whole, which is shorter than its diff:
```python
import functools
import math

import jax
import jax.numpy as jnp
import numpy as np
from jax import lax
from jax.experimental import pallas as pl
from jax.experimental.pallas import tpu as pltpu
from jax.sharding import PartitionSpec as P

AXES = ("row", "col")
ANY = pl.BlockSpec(memory_space=pl.ANY)
HBM = pl.BlockSpec(memory_space=pltpu.HBM)
VMEM = pl.BlockSpec(memory_space=pltpu.VMEM)

CHIPS = 8
ORDER = (
    "first_1",
    "first_2",
    "first_3",
    "first_4",
    "swap_0",
    "second_1",
    "second_2",
    "second_3",
    "tile",
    "swap_1_2_3",
    "chips_0_1_2",
    "swap_4",
    "chips_3_-1_-2_-3",
    "chips_4",
)
AFTER = {"swap_4": ("chips_0_1_2",), "second_1": ("own",)}
COST = {"chips_0_1_2": 64}


def chip_ring(mesh):
    n_row, n_col = mesh.devices.shape
    row_of = {}
    for r in range(n_row):
        for c in range(n_col):
            d = mesh.devices[r, c]
            row_of[(*d.coords, d.core_on_chip)] = (r, c)
    chips = sorted({k[:3] for k, (_, c) in row_of.items() if c == 0})
    if len(chips) * 2 != n_row:
        return None
    spans = [sorted({k[a] for k in chips}) for a in range(3)]
    wide = [a for a in range(3) if len(spans[a]) > 1]
    if len(wide) != 2 or math.prod(len(s) for s in spans) != len(chips):
        return None
    short, long = sorted(wide, key=lambda a: len(spans[a]))
    if len(spans[short]) != 2:
        return None
    lo, hi = spans[short]
    order = [(lo, v) for v in spans[long]] + [(hi, v) for v in reversed(spans[long])]
    place = {sv: i for i, sv in enumerate(order)}
    n = len(order)
    position = np.zeros((n_row, n_col), np.int32)
    core = np.zeros((n_row, n_col), np.int32)
    flat = {}
    for k, (r, c) in row_of.items():
        position[r, c] = place[(k[short], k[long])]
        core[r, c] = k[3]
        flat[(position[r, c], core[r, c], c)] = r * n_col + c
    slot = np.zeros((n_col, n), np.int32)
    for (p, k, c), f in flat.items():
        r = f // n_col
        if r % 2 != k:
            return None
        slot[c, p] = r // 2
    if (slot != slot[:1]).any():
        return None
    return n, position, core, flat, slot[0]


def contribution_kernel(parts, owner_ref, occ_ref, vir_ref, *refs):
    n_col = len(refs) - 3
    outs, (occ, vir, sem) = refs[:n_col], refs[n_col:]
    me = lax.axis_index("col")
    pairs, rows = occ.shape[0], occ.shape[1] // parts

    def fetch(i, ref, buf, k):
        at = pl.ds(i * rows, rows)
        return pltpu.make_async_copy(ref.at[:, at], buf.at[:, at], sem.at[i, k])

    for i in range(parts):
        fetch(i, occ_ref, occ, 0).start()
        fetch(i, vir_ref, vir, 1).start()
    for i in range(parts):
        fetch(i, occ_ref, occ, 0).wait()
        fetch(i, vir_ref, vir, 1).wait()
        at = pl.ds(i * rows, rows)
        pol = [occ[p, at].astype(jnp.float32) * vir[p, at].astype(jnp.float32) for p in range(pairs)]
        for k in range(n_col):
            column = lax.rem(me + k, n_col)
            total = jnp.where(owner_ref[0] == column, pol[0], 0.0)
            for p in range(1, pairs):
                total = total + jnp.where(owner_ref[p] == column, pol[p], 0.0)
            outs[k][at] = total.astype(outs[k].dtype)


def contributions(g_occupied, g_virtual, owner, n_col):
    pairs, rows, depth = g_occupied.shape
    parts = 4
    return pl.pallas_call(
        functools.partial(contribution_kernel, parts),
        out_shape=[jax.ShapeDtypeStruct((rows, depth), jnp.bfloat16)] * n_col,
        in_specs=[pl.BlockSpec(memory_space=pltpu.SMEM), HBM, HBM],
        out_specs=[VMEM] * n_col,
        scratch_shapes=[
            pltpu.VMEM(g_occupied.shape, g_occupied.dtype),
            pltpu.VMEM(g_virtual.shape, g_virtual.dtype),
            pltpu.SemaphoreType.DMA((parts, 2)),
        ],
        cost_estimate=pl.CostEstimate(
            flops=4 * pairs * rows * depth, bytes_accessed=4 * pairs * rows * depth, transcendentals=0
        ),
        name="contributions",
    )(owner.reshape(-1), g_occupied, g_virtual)


def columns_kernel(plan, parts, n_pieces, first, *refs):
    if first:
        own_ref, recv_ref, refs = refs[0], refs[1], refs[2:]
    else:
        tile_ref, refs = refs[0], refs[1:]
    pieces, refs = refs[:n_pieces], refs[n_pieces:]
    if first:
        out_ref, tile_ref, panel, block, sem = refs
    else:
        _, out_ref, panel, block, sem = refs
    shard = panel.shape[2]
    width = 2 * shard
    rows = block.shape[1] // parts
    device = lax.axis_index("row")
    core = lax.rem(device, 2)

    def put(j, i):
        slot = plan[j][0][0]
        for r, s in enumerate(plan[j][0]):
            slot = jnp.where(device == r, s, slot)
        at = pl.multiple_of(slot * width, width)
        span = pl.ds(i * rows, rows)
        return pltpu.make_async_copy(block.at[j, span], out_ref.at[span, pl.ds(at, width)], sem.at[j, i])

    if first:
        total = own_ref[...].astype(jnp.float32) + recv_ref[...].astype(jnp.float32)
        tile_ref[...] = total.astype(tile_ref.dtype)
    for j, (_, here, there) in enumerate(plan):
        panel[j, core] = pieces[here[0]][pl.ds(here[1], shard)]
        panel[j, 1 - core] = pieces[there[0]][pl.ds(there[1], shard)]
        pair = panel[j].reshape(width, panel.shape[3])
        for i in range(parts):
            span = pl.ds(i * rows, rows)
            block[j, span] = lax.dot_general(
                tile_ref[span], pair, (((1,), (1,)), ((), ())), preferred_element_type=jnp.float32
            ).astype(block.dtype)
            put(j, i).start()
    for j in range(len(plan)):
        for i in range(parts):
            put(j, i).wait()


def columns(plan, parts, tile_parts, pieces, shard, out, out_width, cost):
    first = out is None
    rows, depth = tile_parts[0].shape
    out_shape = [jax.ShapeDtypeStruct((rows, out_width), jnp.bfloat16)]
    out_specs = [ANY]
    if first:
        out_shape.append(jax.ShapeDtypeStruct((rows, depth), jnp.bfloat16))
        out_specs.append(VMEM)
    args = [*tile_parts, *pieces] + ([] if first else [out])
    width = 2 * shard
    result = pl.pallas_call(
        functools.partial(columns_kernel, plan, parts, len(pieces), first),
        out_shape=out_shape,
        in_specs=[VMEM] * (len(tile_parts) + len(pieces)) + [ANY] * (not first),
        out_specs=out_specs,
        scratch_shapes=[
            pltpu.VMEM((len(plan), 2, shard, depth), jnp.bfloat16),
            pltpu.VMEM((len(plan), rows, width), jnp.bfloat16),
            pltpu.SemaphoreType.DMA((len(plan), parts)),
        ],
        input_output_aliases={} if first else {len(args) - 1: 0},
        compiler_params=pltpu.CompilerParams(vmem_limit_bytes=24 << 20),
        cost_estimate=pl.CostEstimate(
            flops=cost * 2 * rows * depth * len(plan) * width,
            bytes_accessed=cost * len(plan) * width * rows * 2,
            transcendentals=0,
        ),
        name="columns",
    )(*args)
    return result if first else result[0]


def after(x, *done):
    return lax.optimization_barrier((x, *done))[0]


def ring_body(ring, g_occupied, g_virtual, owner, coulomb):
    n_chips, position, core, flat, slot = ring
    n_row, n_col = position.shape
    half = n_chips // 2

    def pairs(step):
        out = []
        for r in range(n_row):
            for c in range(n_col):
                p, k = step(int(position[r, c]), int(core[r, c]))
                out.append((r * n_col + c, flat[(p % n_chips, k, c)]))
        return out

    onward = pairs(lambda p, k: (p + 1 - 2 * k, k))
    across = pairs(lambda p, k: (p, 1 - k))
    over = [(r * n_col + c, r * n_col + 1 - c) for r in range(n_row) for c in range(n_col)]

    def places(step):
        out = []
        for r in range(n_row):
            p, way = int(position[r, 0]), 1 - 2 * int(core[r, 0])
            out.append(int(slot[(p - way * step) % n_chips]))
        return out

    own, other = contributions(g_occupied, g_virtual, owner, n_col)
    mine = coulomb.T
    shard = mine.shape[0]
    first, second, swapped = {0: mine}, {}, {}
    got = {"own": own}
    out, tile = None, None

    def moved(x, name, way):
        with jax.named_scope(name):
            got[name] = lax.ppermute(after(x, *(got[n] for n in AFTER.get(name, ()))), AXES, way)
        return got[name]

    for name in ORDER:
        kind, *rest = name.split("_")
        steps = [int(i) for i in rest]
        if kind == "first":
            first[steps[0]] = moved(first[steps[0] - 1], name, onward)
        elif kind == "second":
            second[steps[0]] = moved(second[steps[0] - 1], name, onward)
        elif kind == "tile":
            received = moved(other, name, over)
        elif kind == "swap":
            if steps == [0]:
                second[0] = moved(mine, name, across)
                continue
            parts = [x[i] for i in steps for x in ((first, second) if i < half else (first,))]
            both = moved(jnp.concatenate(parts), name, across)
            for n, i in enumerate(steps):
                swapped[i] = (both, 2 * n * shard)
        else:
            pieces, plan = [], []

            def add(x):
                if not any(x is y for y in pieces):
                    pieces.append(x)
                return next(n for n, y in enumerate(pieces) if x is y)

            for i in steps:
                if i == half:
                    plan.append((places(i), (add(first[i]), 0), (add(swapped[i][0]), swapped[i][1])))
                elif i >= 0:
                    plan.append((places(i), (add(first[i]), 0), (add(second[i]), 0)))
                else:
                    both, at = swapped[-i]
                    plan.append((places(i), (add(both), at + shard), (add(both), at)))
            parts = 4 if half in steps else 1
            terms = [own, received] if tile is None else [tile]
            result = columns(plan, parts, terms, pieces, shard, out, n_row * shard, COST.get(name, 1))
            if tile is None:
                result, tile = result
            out = result
            got[name] = tile if len(terms) == 2 else out
    return out


def gather_body(g_occupied, g_virtual, owner, coulomb):
    n_col = lax.axis_size("col")
    pol = g_occupied.astype(jnp.float32) * g_virtual.astype(jnp.float32)
    columns = jnp.arange(n_col, dtype=jnp.int32)
    onehot = (owner[:, 0][:, None] == columns[None, :]).astype(jnp.float32)
    contrib = jnp.einsum("sd,sij->dij", onehot, pol).astype(jnp.bfloat16)
    received = lax.all_to_all(contrib, "col", split_axis=0, concat_axis=0, tiled=True)
    tile = jnp.sum(received.astype(jnp.float32), axis=0).astype(jnp.bfloat16)
    panel = lax.all_gather(coulomb, "row", axis=1, tiled=True)
    return jnp.dot(tile, panel, preferred_element_type=jnp.float32).astype(jnp.bfloat16)


def solution(mesh):
    ring = chip_ring(mesh) if mesh.shape["col"] == 2 else None
    if ring and ring[0] != CHIPS:
        ring = None
    return jax.shard_map(
        functools.partial(ring_body, ring) if ring else gather_body,
        mesh=mesh,
        in_specs=(P(AXES, None, None), P(AXES, None, None), P(AXES, None), P("col", "row")),
        out_specs=P(AXES, None),
        check_vma=False,
    )
```

time: 70.2 us -> 29.9 us (0.43)
  waiting for transfers between devices: 29.2 us -> 6.45 us
  blocking collectives: 17.6 us -> 0 us
  starting transfers between devices: 0.01 us -> 14.6 us
  between operations: 13.4 us -> 0.11 us
  Pallas kernels: 0 us -> 8.55 us
  matrix products: 7.25 us -> 0 us
  other arithmetic: 2.32 us -> 0 us
    all_gather x1 -> x0, waiting for transfers between devices: 28.5 us -> none  [body(): lax.all_gather(coulomb, 'row', axis=1, tiled=True)]
    all_to_all x1 -> x0, blocking collectives: 17.6 us -> none  [body(): lax.all_to_all(contrib, 'col', split_axis=0, concat_axis=0, tiled=True)]
    ppermute x0 -> x11, starting transfers between devices: none -> 14.6 us  [moved(): lax.ppermute(after(x, *(got[n] for n in AFTER.get(name, ()))), AXES, way)]
    pallas_call x0 -> x4, Pallas kernels: none -> 8.55 us  [the longest x3 5.26 us: columns(): pl.pallas_call(functools.partial(columns_kernel, plan, parts, len(pieces)...]
    dot_general x2 -> x0, matrix products: 7.25 us -> none  [the longest x1 5.38 us: body(): jnp.dot(tile, lax.all_gather(coulomb, 'row', axis=1, tiled=True), preferr...]
    ppermute x0 -> x11, waiting for transfers between devices: none -> 6.45 us  [moved(): lax.ppermute(after(x, *(got[n] for n in AFTER.get(name, ()))), AXES, way)]
    mul x1 -> x0, other arithmetic: 1.83 us -> none  [body(): pol = g_occupied.astype(jnp.float32) * g_virtual.astype(jnp.float32)]
    unnamed x1 -> x0, waiting for transfers between devices: 0.71 us -> none
  transfers between devices with their start and end apart: 1 -> 11, of which waited for: 1 -> 7; matrix products, arithmetic and copies ran while one was open for 6% -> 0% of each run, Pallas kernels for 0% -> 24%
where the time goes in v2:
time: 29.9 us; the launch traced here: 29.8 us
  starting transfers between devices  14.6 us (49%)
  Pallas kernels  8.55 us (29%)
  waiting for transfers between devices  6.45 us (22%)
    ppermute x11, starting transfers between devices, moved(): lax.ppermute(after(x, *(got[n] for n in AFTER.get(name, ()))), AXES, way)  14.6 us
    ppermute x11, waiting for transfers between devices, moved(): lax.ppermute(after(x, *(got[n] for n in AFTER.get(name, ()))), AXES, way)  6.45 us
    pallas_call x3, Pallas kernels, columns(): pl.pallas_call(functools.partial(columns_kernel, plan, parts, len(pieces)...  5.26 us
    pallas_call x1, Pallas kernels, contributions(): pl.pallas_call(functools.partial(contribution_kernel, parts), out_shape=[...  3.28 us
  transfers between devices with their start and end apart: 11, of which 7 were waited for; matrix products, arithmetic and copies ran while one was open for 0% of the time, Pallas kernels for 24%

profile of v2, /device:TPU:0, one launch (start us, length us, event | category | flops | bytes accessed | tf_op | source)
XLA Modules:
  0.0 29.8 jit_solution(17093135589595645811)
XLA Ops:
  0.0 0.5 %collective-permute-start.1 = (bf16[192,512]{1,0:T(8,128)(2,1)}, bf16[192,512]{1,0:T(8,128)(2,1)S(1)}, u32[]{:S(2)}, u32[]{:S(2)}) collective-permute-start(bf16[192,512]{1,0:T(8,128)(2,1)} %bitcast.2), channel_id=1, source_target_pairs={{0,2},{1,3},{2,0},{3,1},{4,6},{5,7},{6,4},{7,5},{8,10},{9,11},{10,... | collective-permute-start | bytes 589832 | tf_op jit(solution)/shard_map/swap_0/ppermute | solution.py:234
  0.5 2.6 %collective-permute-start.2 = (bf16[192,512]{1,0:T(8,128)(2,1)}, bf16[192,512]{1,0:T(8,128)(2,1)S(1)}, u32[]{:S(2)}, u32[]{:S(2)}) collective-permute-start(bf16[192,512]{1,0:T(8,128)(2,1)} %bitcast.3), channel_id=1, source_target_pairs={{0,8},{1,9},{2,6},{3,7},{4,0},{5,1},{6,14},{7,15},{8,16},{9,17},{1... | collective-permute-start | bytes 589832 | tf_op jit(solution)/shard_map/first_1/ppermute | solution.py:234
  3.0 3.3 %contributions.1 = (bf16[512,512]{1,0:T(8,128)(2,1)}, bf16[512,512]{1,0:T(8,128)(2,1)}) custom-call(s32[2]{0:T(128)} %bitcast.5, bf16[2,512,512]{2,1,0:T(8,128)(2,1)} %occ_ref.1, bf16[2,512,512]{2,1,0:T(8,128)(2,1)} %vir_ref.1), custom_call_target="tpu_custom_call" | custom-call | flops 2097152 | bytes 2097152 | tf_op jit(solution)/shard_map/contributions/pallas_call | solution.py:106
  6.3 0.0 collective-permute-done.1.refs_3_
  6.3 1.6 %collective-permute-start.3 = (bf16[192,512]{1,0:T(8,128)(2,1)S(1)}, bf16[192,512]{1,0:T(8,128)(2,1)S(1)}, u32[]{:S(2)}, u32[]{:S(2)}) collective-permute-start(bf16[192,512]{1,0:T(8,128)(2,1)S(1)} %collective-permute-done.1.refs_3_), channel_id=1, source_target_pairs={{0,8},{1,9},{2,6},{3,7},{4,0},{5,1},{6,14},{7,15},{8,16},{9,17},{1... | collective-permute-start | bytes 589832 | tf_op jit(solution)/shard_map/second_1/ppermute | solution.py:234
  8.0 1.6 %collective-permute-start.4 = (bf16[192,512]{1,0:T(8,128)(2,1)S(1)}, bf16[192,512]{1,0:T(8,128)(2,1)S(1)}, u32[]{:S(2)}, u32[]{:S(2)}) collective-permute-start(bf16[192,512]{1,0:T(8,128)(2,1)S(1)} %collective-permute-done.2.refs_4_), channel_id=1, source_target_pairs={{0,8},{1,9},{2,6},{3,7},{4,0},{5,1},{6,14},{7,15},{8,16},{9,17},{1... | collective-permute-start | bytes 589832 | tf_op jit(solution)/shard_map/first_2/ppermute | solution.py:234
  9.5 1.5 %collective-permute-start = (bf16[512,512]{1,0:T(8,128)(2,1)}, bf16[512,512]{1,0:T(8,128)(2,1)S(1)}, u32[]{:S(2)}, u32[]{:S(2)}) collective-permute-start(bf16[512,512]{1,0:T(8,128)(2,1)} %get-tuple-element.12), channel_id=1, source_target_pairs={{0,1},{1,0},{2,3},{3,2},{4,5},{5,4},{6,7},{7,6},{8,9},{9,8},{10,11... | collective-permute-start | bytes 1572872 | tf_op jit(solution)/shard_map/tile/ppermute | solution.py:234
  11.1 1.0 %collective-permute-done.3.refs_5_ = bf16[192,512]{1,0:T(8,128)(2,1)S(1)} collective-permute-done((bf16[192,512]{1,0:T(8,128)(2,1)S(1)}, bf16[192,512]{1,0:T(8,128)(2,1)S(1)}, u32[]{:S(2)}, u32[]{:S(2)}) %collective-permute-start.3) | collective-permute-done | bytes 196640 | tf_op jit(solution)/shard_map/second_1/ppermute | solution.py:234
  12.1 1.6 %collective-permute-start.5 = (bf16[192,512]{1,0:T(8,128)(2,1)S(1)}, bf16[192,512]{1,0:T(8,128)(2,1)S(1)}, u32[]{:S(2)}, u32[]{:S(2)}) collective-permute-start(bf16[192,512]{1,0:T(8,128)(2,1)S(1)} %collective-permute-done.3.refs_5_), channel_id=1, source_target_pairs={{0,8},{1,9},{2,6},{3,7},{4,0},{5,1},{6,14},{7,15},{8,16},{9,17},{1... | collective-permute-start | bytes 589832 | tf_op jit(solution)/shard_map/second_2/ppermute | solution.py:234
  13.6 0.5 %collective-permute-done.4.refs_6_ = bf16[192,512]{1,0:T(8,128)(2,1)S(1)} collective-permute-done((bf16[192,512]{1,0:T(8,128)(2,1)S(1)}, bf16[192,512]{1,0:T(8,128)(2,1)S(1)}, u32[]{:S(2)}, u32[]{:S(2)}) %collective-permute-start.4) | collective-permute-done | bytes 196640 | tf_op jit(solution)/shard_map/first_2/ppermute | solution.py:234
  14.2 1.6 %collective-permute-start.6 = (bf16[192,512]{1,0:T(8,128)(2,1)S(1)}, bf16[192,512]{1,0:T(8,128)(2,1)S(1)}, u32[]{:S(2)}, u32[]{:S(2)}) collective-permute-start(bf16[192,512]{1,0:T(8,128)(2,1)S(1)} %collective-permute-done.4.refs_6_), channel_id=1, source_target_pairs={{0,8},{1,9},{2,6},{3,7},{4,0},{5,1},{6,14},{7,15},{8,16},{9,17},{1... | collective-permute-start | bytes 589832 | tf_op jit(solution)/shard_map/first_3/ppermute | solution.py:234
  15.8 1.9 %collective-permute-done.5.refs_7_ = bf16[192,512]{1,0:T(8,128)(2,1)S(1)} collective-permute-done((bf16[192,512]{1,0:T(8,128)(2,1)S(1)}, bf16[192,512]{1,0:T(8,128)(2,1)S(1)}, u32[]{:S(2)}, u32[]{:S(2)}) %collective-permute-start.5) | collective-permute-done | bytes 196640 | tf_op jit(solution)/shard_map/second_2/ppermute | solution.py:234
  17.7 1.6 %collective-permute-start.9 = (bf16[192,512]{1,0:T(8,128)(2,1)S(1)}, bf16[192,512]{1,0:T(8,128)(2,1)S(1)}, u32[]{:S(2)}, u32[]{:S(2)}) collective-permute-start(bf16[192,512]{1,0:T(8,128)(2,1)S(1)} %collective-permute-done.5.refs_7_), channel_id=1, source_target_pairs={{0,8},{1,9},{2,6},{3,7},{4,0},{5,1},{6,14},{7,15},{8,16},{9,17},{1... | collective-permute-start | bytes 589832 | tf_op jit(solution)/shard_map/second_3/ppermute | solution.py:234
  19.3 0.5 %collective-permute-done.6.refs_1_ = bf16[192,512]{1,0:T(8,128)(2,1)S(1)} collective-permute-done((bf16[192,512]{1,0:T(8,128)(2,1)S(1)}, bf16[192,512]{1,0:T(8,128)(2,1)S(1)}, u32[]{:S(2)}, u32[]{:S(2)}) %collective-permute-start.6) | collective-permute-done | bytes 196640 | tf_op jit(solution)/shard_map/first_3/ppermute | solution.py:234
  19.8 1.6 %collective-permute-start.7 = (bf16[192,512]{1,0:T(8,128)(2,1)S(1)}, bf16[192,512]{1,0:T(8,128)(2,1)S(1)}, u32[]{:S(2)}, u32[]{:S(2)}) collective-permute-start(bf16[192,512]{1,0:T(8,128)(2,1)S(1)} %collective-permute-done.6.refs_1_), channel_id=1, source_target_pairs={{0,8},{1,9},{2,6},{3,7},{4,0},{5,1},{6,14},{7,15},{8,16},{9,17},{1... | collective-permute-start | bytes 589832 | tf_op jit(solution)/shard_map/first_4/ppermute | solution.py:234
  21.4 1.9 %collective-permute-done.9.refs_2_ = bf16[192,512]{1,0:T(8,128)(2,1)S(1)} collective-permute-done((bf16[192,512]{1,0:T(8,128)(2,1)S(1)}, bf16[192,512]{1,0:T(8,128)(2,1)S(1)}, u32[]{:S(2)}, u32[]{:S(2)}) %collective-permute-start.9) | collective-permute-done | bytes 196640 | tf_op jit(solution)/shard_map/second_3/ppermute | solution.py:234
  23.4 0.1 collective-permute-start.10
  23.5 0.0 collective-permute-done.refs_1_
  23.5 1.8 %columns.3 = (bf16[512,3072]{1,0:T(8,128)(2,1)}, bf16[512,512]{1,0:T(8,128)(2,1)S(1)}) custom-call(bf16[512,512]{1,0:T(8,128)(2,1)S(1)} %copy-done, bf16[512,512]{1,0:T(8,128)(2,1)S(1)} %collective-permute-done.refs_1_, bf16[192,512]{1,0:T(8,128)(2,1)S(1)} %bitcast.4, bf16[192,512]{1,0:T(8,128)(2,1)S(1)} %collective-permute-done.1.refs_3_, ...), custom_call_target="tpu_custom_call" | custom-call | flops 38654705664 | bytes 75497472 | tf_op jit(solution)/shard_map/columns/pallas_call | solution.py:175
  25.4 0.1 collective-permute-done.7.refs_1_
  25.5 0.4 %collective-permute-start.8 = (bf16[192,512]{1,0:T(8,128)(2,1)S(1)}, bf16[192,512]{1,0:T(8,128)(2,1)S(1)}, u32[]{:S(2)}, u32[]{:S(2)}) collective-permute-start(bf16[192,512]{1,0:T(8,128)(2,1)S(1)} %collective-permute-done.7.refs_1_), channel_id=1, source_target_pairs={{0,2},{1,3},{2,0},{3,1},{4,6},{5,7},{6,4},{7,5},{8,10},{9,11},{10,... | collective-permute-start | bytes 589832 | tf_op jit(solution)/shard_map/swap_4/ppermute | solution.py:234
  25.9 0.4 %collective-permute-done.10.refs_3_ = bf16[1152,512]{1,0:T(8,128)(2,1)S(1)} collective-permute-done((bf16[1152,512]{1,0:T(8,128)(2,1)S(1)}, bf16[1152,512]{1,0:T(8,128)(2,1)S(1)}, u32[]{:S(2)}, u32[]{:S(2)}) %collective-permute-start.10) | collective-permute-done | bytes 1179680 | tf_op jit(solution)/shard_map/swap_1_2_3/ppermute | solution.py:234
  26.3 2.1 %columns.4.refs_3_ = bf16[512,3072]{1,0:T(8,128)(2,1)} custom-call(bf16[512,512]{1,0:T(8,128)(2,1)S(1)} %get-tuple-element.14.refs_0_, bf16[192,512]{1,0:T(8,128)(2,1)S(1)} %collective-permute-done.6.refs_1_, bf16[192,512]{1,0:T(8,128)(2,1)S(1)} %collective-permute-done.9.refs_2_, ...), custom_call_target="tpu_custom_call", output_to_operand_aliasing={{}: (4, {})} | custom-call | flops 805306368 | bytes 1572864 | tf_op jit(solution)/shard_map/columns/pallas_call | solution.py:175
  28.4 1.3 %columns.5 = bf16[512,3072]{1,0:T(8,128)(2,1)} custom-call(bf16[512,512]{1,0:T(8,128)(2,1)S(1)} %get-tuple-element.14.refs_0_, bf16[192,512]{1,0:T(8,128)(2,1)S(1)} %collective-permute-done.7.refs_1_, bf16[192,512]{1,0:T(8,128)(2,1)S(1)} %collective-permute-done.8.refs_2_, bf16[512,3072]{1,0:T(8,128)(2,1)} %columns.4.refs_3_), custom_call_target="tpu_custom_call", output_to_operand_aliasing={{}: (3, {})} | custom-call | flops 201326592 | bytes 393216 | tf_op jit(solution)/shard_map/columns/pallas_call | solution.py:175
  (12 shorter events, 0.1 us)
Async XLA Ops:
  0.0 6.3 %collective-permute-start.1 = (bf16[192,512]{1,0:T(8,128)(2,1)}, bf16[192,512]{1,0:T(8,128)(2,1)S(1)}, u32[]{:S(2)}, u32[]{:S(2)}) collective-permute-start(bf16[192,512]{1,0:T(8,128)(2,1)} %bitcast.2), channel_id=1, source_target_pairs={{0,2},{1,3},{2,0},{3,1},{4,6},{5,7},{6,4},{7,5},{8,10},{9,11},{10,... | collective-permute-start | bytes 589832 | tf_op jit(solution)/shard_map/swap_0/ppermute | solution.py:234
  0.5 7.5 %collective-permute-start.2 = (bf16[192,512]{1,0:T(8,128)(2,1)}, bf16[192,512]{1,0:T(8,128)(2,1)S(1)}, u32[]{:S(2)}, u32[]{:S(2)}) collective-permute-start(bf16[192,512]{1,0:T(8,128)(2,1)} %bitcast.3), channel_id=1, source_target_pairs={{0,8},{1,9},{2,6},{3,7},{4,0},{5,1},{6,14},{7,15},{8,16},{9,17},{1... | collective-permute-start | bytes 589832 | tf_op jit(solution)/shard_map/first_1/ppermute | solution.py:234
  6.3 5.7 %collective-permute-start.3 = (bf16[192,512]{1,0:T(8,128)(2,1)S(1)}, bf16[192,512]{1,0:T(8,128)(2,1)S(1)}, u32[]{:S(2)}, u32[]{:S(2)}) collective-permute-start(bf16[192,512]{1,0:T(8,128)(2,1)S(1)} %collective-permute-done.1.refs_3_), channel_id=1, source_target_pairs={{0,8},{1,9},{2,6},{3,7},{4,0},{5,1},{6,14},{7,15},{8,16},{9,17},{1... | collective-permute-start | bytes 589832 | tf_op jit(solution)/shard_map/second_1/ppermute | solution.py:234
  8.0 6.2 %collective-permute-start.4 = (bf16[192,512]{1,0:T(8,128)(2,1)S(1)}, bf16[192,512]{1,0:T(8,128)(2,1)S(1)}, u32[]{:S(2)}, u32[]{:S(2)}) collective-permute-start(bf16[192,512]{1,0:T(8,128)(2,1)S(1)} %collective-permute-done.2.refs_4_), channel_id=1, source_target_pairs={{0,8},{1,9},{2,6},{3,7},{4,0},{5,1},{6,14},{7,15},{8,16},{9,17},{1... | collective-permute-start | bytes 589832 | tf_op jit(solution)/shard_map/first_2/ppermute | solution.py:234
  9.5 14.0 %copy-start = (bf16[512,512]{1,0:T(8,128)(2,1)S(1)}, bf16[512,512]{1,0:T(8,128)(2,1)}, u32[]{:S(2)}) copy-start(bf16[512,512]{1,0:T(8,128)(2,1)} %get-tuple-element.11.refs_0_) | copy-start | bytes 1572868
  9.5 14.0 %copy-start.1 = (bf16[512,192]{0,1:T(8,128)(2,1)S(1)}, bf16[512,192]{0,1:T(8,128)(2,1)}, u32[]{:S(2)}) copy-start(bf16[512,192]{0,1:T(8,128)(2,1)} %param.7) | copy-start | bytes 589828
  9.5 13.9 %collective-permute-start = (bf16[512,512]{1,0:T(8,128)(2,1)}, bf16[512,512]{1,0:T(8,128)(2,1)S(1)}, u32[]{:S(2)}, u32[]{:S(2)}) collective-permute-start(bf16[512,512]{1,0:T(8,128)(2,1)} %get-tuple-element.12), channel_id=1, source_target_pairs={{0,1},{1,0},{2,3},{3,2},{4,5},{5,4},{6,7},{7,6},{8,9},{9,8},{10,11... | collective-permute-start | bytes 1572872 | tf_op jit(solution)/shard_map/tile/ppermute | solution.py:234
  12.1 5.7 %collective-permute-start.5 = (bf16[192,512]{1,0:T(8,128)(2,1)S(1)}, bf16[192,512]{1,0:T(8,128)(2,1)S(1)}, u32[]{:S(2)}, u32[]{:S(2)}) collective-permute-start(bf16[192,512]{1,0:T(8,128)(2,1)S(1)} %collective-permute-done.3.refs_5_), channel_id=1, source_target_pairs={{0,8},{1,9},{2,6},{3,7},{4,0},{5,1},{6,14},{7,15},{8,16},{9,17},{1... | collective-permute-start | bytes 589832 | tf_op jit(solution)/shard_map/second_2/ppermute | solution.py:234
  14.2 5.7 %collective-permute-start.6 = (bf16[192,512]{1,0:T(8,128)(2,1)S(1)}, bf16[192,512]{1,0:T(8,128)(2,1)S(1)}, u32[]{:S(2)}, u32[]{:S(2)}) collective-permute-start(bf16[192,512]{1,0:T(8,128)(2,1)S(1)} %collective-permute-done.4.refs_6_), channel_id=1, source_target_pairs={{0,8},{1,9},{2,6},{3,7},{4,0},{5,1},{6,14},{7,15},{8,16},{9,17},{1... | collective-permute-start | bytes 589832 | tf_op jit(solution)/shard_map/first_3/ppermute | solution.py:234
  17.7 5.7 %collective-permute-start.9 = (bf16[192,512]{1,0:T(8,128)(2,1)S(1)}, bf16[192,512]{1,0:T(8,128)(2,1)S(1)}, u32[]{:S(2)}, u32[]{:S(2)}) collective-permute-start(bf16[192,512]{1,0:T(8,128)(2,1)S(1)} %collective-permute-done.5.refs_7_), channel_id=1, source_target_pairs={{0,8},{1,9},{2,6},{3,7},{4,0},{5,1},{6,14},{7,15},{8,16},{9,17},{1... | collective-permute-start | bytes 589832 | tf_op jit(solution)/shard_map/second_3/ppermute | solution.py:234
  19.8 5.7 %collective-permute-start.7 = (bf16[192,512]{1,0:T(8,128)(2,1)S(1)}, bf16[192,512]{1,0:T(8,128)(2,1)S(1)}, u32[]{:S(2)}, u32[]{:S(2)}) collective-permute-start(bf16[192,512]{1,0:T(8,128)(2,1)S(1)} %collective-permute-done.6.refs_1_), channel_id=1, source_target_pairs={{0,8},{1,9},{2,6},{3,7},{4,0},{5,1},{6,14},{7,15},{8,16},{9,17},{1... | collective-permute-start | bytes 589832 | tf_op jit(solution)/shard_map/first_4/ppermute | solution.py:234
  23.4 2.9 %collective-permute-start.10 = (bf16[1152,512]{1,0:T(8,128)(2,1)S(1)}, bf16[1152,512]{1,0:T(8,128)(2,1)S(1)}, u32[]{:S(2)}, u32[]{:S(2)}) collective-permute-start(bf16[1152,512]{1,0:T(8,128)(2,1)S(1)} %constant_dynamic-update-slice_fusion), channel_id=1, source_target_pairs={{0,2},{1,3},{2,0},{3,1},{4,6},{5,7},{6,4},{7,5},{8,10},{9,11},{10,... | collective-permute-start | bytes 3538952 | tf_op jit(solution)/shard_map/swap_1_2_3/ppermute | solution.py:234
  25.5 2.9 %collective-permute-start.8 = (bf16[192,512]{1,0:T(8,128)(2,1)S(1)}, bf16[192,512]{1,0:T(8,128)(2,1)S(1)}, u32[]{:S(2)}, u32[]{:S(2)}) collective-permute-start(bf16[192,512]{1,0:T(8,128)(2,1)S(1)} %collective-permute-done.7.refs_1_), channel_id=1, source_target_pairs={{0,2},{1,3},{2,0},{3,1},{4,6},{5,7},{6,4},{7,5},{8,10},{9,11},{10,... | collective-permute-start | bytes 589832 | tf_op jit(solution)/shard_map/swap_4/ppermute | solution.py:234

commit v3 on v2

--- a/solution.py
+++ b/solution.py
@@ -25,14 +25,16 @@
     "second_2",
     "second_3",
     "tile",
-    "swap_1_2_3",
-    "chips_0_1_2",
+    "swap_1_2",
+    "swap_3",
+    "chips_0_1",
     "swap_4",
-    "chips_3_-1_-2_-3",
+    "chips_2_3_-1_-2_-3",
     "chips_4",
 )
-AFTER = {"swap_4": ("chips_0_1_2",), "second_1": ("own",)}
-COST = {"chips_0_1_2": 64}
+AFTER = {"swap_4": ("chips_0_1",), "second_1": ("own",)}
+COST = {"chips_0_1": 16}
+FRONT = 3221225472
 
 
 def chip_ring(mesh):
@@ -74,116 +76,140 @@
     return n, position, core, flat, slot[0]
 
 
-def contribution_kernel(parts, owner_ref, occ_ref, vir_ref, *refs):
-    n_col = len(refs) - 3
-    outs, (occ, vir, sem) = refs[:n_col], refs[n_col:]
-    me = lax.axis_index("col")
-    pairs, rows = occ.shape[0], occ.shape[1] // parts
-
-    def fetch(i, ref, buf, k):
-        at = pl.ds(i * rows, rows)
-        return pltpu.make_async_copy(ref.at[:, at], buf.at[:, at], sem.at[i, k])
-
-    for i in range(parts):
-        fetch(i, occ_ref, occ, 0).start()
-        fetch(i, vir_ref, vir, 1).start()
-    for i in range(parts):
-        fetch(i, occ_ref, occ, 0).wait()
-        fetch(i, vir_ref, vir, 1).wait()
-        at = pl.ds(i * rows, rows)
-        pol = [occ[p, at].astype(jnp.float32) * vir[p, at].astype(jnp.float32) for p in range(pairs)]
-        for k in range(n_col):
-            column = lax.rem(me + k, n_col)
-            total = jnp.where(owner_ref[0] == column, pol[0], 0.0)
-            for p in range(1, pairs):
-                total = total + jnp.where(owner_ref[p] == column, pol[p], 0.0)
-            outs[k][at] = total.astype(outs[k].dtype)
-
-
-def contributions(g_occupied, g_virtual, owner, n_col):
+def tile_columns_kernel(n_col, out_ref):
+    row = lax.broadcasted_iota(jnp.int32, out_ref.shape, 0)
+    out_ref[...] = lax.rem(lax.axis_index("col") + row, n_col)
+
+
+def tile_columns(n_col):
+    return pl.pallas_call(
+        functools.partial(tile_columns_kernel, n_col),
+        out_shape=jax.ShapeDtypeStruct((8 * pl.cdiv(n_col, 8), 128), jnp.int32),
+        out_specs=VMEM,
+        cost_estimate=pl.CostEstimate(flops=FRONT, bytes_accessed=1 << 10, transcendentals=0),
+        name="tile_columns",
+    )()
+
+
+def contribution_kernel(owner_ref, column_ref, occ_ref, vir_ref, *outs):
+    pol = [occ_ref[p].astype(jnp.float32) * vir_ref[p].astype(jnp.float32) for p in range(occ_ref.shape[0])]
+    lanes = column_ref.shape[1]
+    for k, out in enumerate(outs):
+        column = column_ref[pl.ds(k, 1)]
+        picked = [jnp.where(owner_ref[:, p : p + 1] == column, 1.0, 0.0).astype(jnp.float32) for p in range(len(pol))]
+        for at in range(0, out.shape[1], lanes):
+            span = slice(at, at + lanes)
+            total = pol[0][:, span] * picked[0]
+            for p in range(1, len(pol)):
+                total = total + pol[p][:, span] * picked[p]
+            out[:, span] = total.astype(out.dtype)
+
+
+def contributions(g_occupied, g_virtual, owner, column, n_col):
     pairs, rows, depth = g_occupied.shape
-    parts = 4
     return pl.pallas_call(
-        functools.partial(contribution_kernel, parts),
+        contribution_kernel,
         out_shape=[jax.ShapeDtypeStruct((rows, depth), jnp.bfloat16)] * n_col,
-        in_specs=[pl.BlockSpec(memory_space=pltpu.SMEM), HBM, HBM],
+        in_specs=[VMEM, VMEM, VMEM, VMEM],
         out_specs=[VMEM] * n_col,
-        scratch_shapes=[
-            pltpu.VMEM(g_occupied.shape, g_occupied.dtype),
-            pltpu.VMEM(g_virtual.shape, g_virtual.dtype),
-            pltpu.SemaphoreType.DMA((parts, 2)),
-        ],
+        compiler_params=pltpu.CompilerParams(vmem_limit_bytes=24 << 20),
         cost_estimate=pl.CostEstimate(
             flops=4 * pairs * rows * depth, bytes_accessed=4 * pairs * rows * depth, transcendentals=0
         ),
         name="contributions",
-    )(owner.reshape(-1), g_occupied, g_virtual)
-
-
-def columns_kernel(plan, parts, n_pieces, first, *refs):
-    if first:
-        own_ref, recv_ref, refs = refs[0], refs[1], refs[2:]
-    else:
-        tile_ref, refs = refs[0], refs[1:]
-    pieces, refs = refs[:n_pieces], refs[n_pieces:]
-    if first:
-        out_ref, tile_ref, panel, block, sem = refs
-    else:
-        _, out_ref, panel, block, sem = refs
-    shard = panel.shape[2]
-    width = 2 * shard
-    rows = block.shape[1] // parts
+    )(owner.reshape(1, pairs), column, g_occupied, g_virtual)
+
+
+def columns_kernel(shape, n_terms, n_pieces, plan, held, last, *refs):
     device = lax.axis_index("row")
     core = lax.rem(device, 2)
-
-    def put(j, i):
-        slot = plan[j][0][0]
-        for r, s in enumerate(plan[j][0]):
+    shard = shape[0]
+    width = 2 * shard
+    refs = list(refs)
+    terms = [refs.pop(0) for _ in range(n_terms)]
+    pieces = [refs.pop(0) for _ in range(n_pieces)]
+    ready = refs.pop(0) if held else None
+    sem, panel = refs.pop(), refs.pop()
+    block = refs.pop()
+    tile = terms[0] if n_terms == 1 else refs.pop()
+    out = refs.pop() if refs else None
+
+    def put(source, place, span, n):
+        slot = place[0]
+        for r, s in enumerate(place):
             slot = jnp.where(device == r, s, slot)
-        at = pl.multiple_of(slot * width, width)
-        span = pl.ds(i * rows, rows)
-        return pltpu.make_async_copy(block.at[j, span], out_ref.at[span, pl.ds(at, width)], sem.at[j, i])
-
-    if first:
-        total = own_ref[...].astype(jnp.float32) + recv_ref[...].astype(jnp.float32)
-        tile_ref[...] = total.astype(tile_ref.dtype)
-    for j, (_, here, there) in enumerate(plan):
+        at = pl.ds(pl.multiple_of(slot * width, width), width)
+        return pltpu.make_async_copy(source.at[span], out.at[span, at], sem.at[n])
+
+    copies = [put(ready.at[j], place, pl.ds(0, tile.shape[0]), j) for j, place in enumerate(held)]
+    for c in copies:
+        c.start()
+    if n_terms == 2:
+        tile[...] = (terms[0][...].astype(jnp.float32) + terms[1][...].astype(jnp.float32)).astype(tile.dtype)
+    parts = 4 if last else 1
+    rows = tile.shape[0] // parts
+    for j, (place, here, there) in enumerate(plan):
         panel[j, core] = pieces[here[0]][pl.ds(here[1], shard)]
         panel[j, 1 - core] = pieces[there[0]][pl.ds(there[1], shard)]
         pair = panel[j].reshape(width, panel.shape[3])
         for i in range(parts):
             span = pl.ds(i * rows, rows)
             block[j, span] = lax.dot_general(
-                tile_ref[span], pair, (((1,), (1,)), ((), ())), preferred_element_type=jnp.float32
+                tile[span], pair, (((1,), (1,)), ((), ())), preferred_element_type=jnp.float32
             ).astype(block.dtype)
-            put(j, i).start()
-    for j in range(len(plan)):
-        for i in range(parts):
-            put(j, i).wait()
-
-
-def columns(plan, parts, tile_parts, pieces, shard, out, out_width, cost):
-    first = out is None
-    rows, depth = tile_parts[0].shape
-    out_shape = [jax.ShapeDtypeStruct((rows, out_width), jnp.bfloat16)]
-    out_specs = [ANY]
-    if first:
+            if last:
+                copies.append(put(block.at[j], place, span, len(copies)))
+                copies[-1].start()
+    for c in copies:
+        c.wait()
+
+
+def columns(plan, terms, pieces, shard, ready, held, out, last, out_width, cost):
+    rows, depth = terms[0].shape
+    width = 2 * shard
+    wide = jax.ShapeDtypeStruct((rows, out_width), jnp.bfloat16)
+    blocks = (len(plan), rows, width)
+    args = [*terms, *pieces]
+    in_specs = [VMEM] * len(args)
+    if held:
+        args.append(ready)
+        in_specs.append(VMEM)
+    aliases = {}
+    if out is not None:
+        aliases = {len(args): 0}
+        args.append(out)
+        in_specs.append(ANY)
+    out_shape, out_specs = [], []
+    if held or last:
+        out_shape.append(wide)
+        out_specs.append(ANY)
+    if len(terms) == 2:
         out_shape.append(jax.ShapeDtypeStruct((rows, depth), jnp.bfloat16))
         out_specs.append(VMEM)
-    args = [*tile_parts, *pieces] + ([] if first else [out])
-    width = 2 * shard
+    if not last:
+        out_shape.append(jax.ShapeDtypeStruct(blocks, jnp.bfloat16))
+        out_specs.append(VMEM)
+    scratch = [pltpu.VMEM(blocks, jnp.bfloat16)] if last else []
+    n_in = len(args)
+
+    def body(*refs):
+        refs = list(refs)
+        if out is not None:
+            del refs[n_in - 1]
+        columns_kernel((shard, width), len(terms), len(pieces), plan, held, last, *refs)
+
     result = pl.pallas_call(
-        functools.partial(columns_kernel, plan, parts, len(pieces), first),
+        body,
         out_shape=out_shape,
-        in_specs=[VMEM] * (len(tile_parts) + len(pieces)) + [ANY] * (not first),
+        in_specs=in_specs,
         out_specs=out_specs,
-        scratch_shapes=[
+        scratch_shapes=scratch
+        + [
             pltpu.VMEM((len(plan), 2, shard, depth), jnp.bfloat16),
-            pltpu.VMEM((len(plan), rows, width), jnp.bfloat16),
-            pltpu.SemaphoreType.DMA((len(plan), parts)),
+            pltpu.SemaphoreType.DMA((len(held) + 4 * len(plan),)),
         ],
-        input_output_aliases={} if first else {len(args) - 1: 0},
-        compiler_params=pltpu.CompilerParams(vmem_limit_bytes=24 << 20),
+        input_output_aliases=aliases,
+        compiler_params=pltpu.CompilerParams(vmem_limit_bytes=16 << 20),
         cost_estimate=pl.CostEstimate(
             flops=cost * 2 * rows * depth * len(plan) * width,
             bytes_accessed=cost * len(plan) * width * rows * 2,
@@ -191,7 +217,10 @@
         ),
         name="columns",
     )(*args)
-    return result if first else result[0]
+    result = list(result)
+    out = result.pop(0) if held or last else None
+    tile = result.pop(0) if len(terms) == 2 else terms[0]
+    return out, None if last else result.pop(0), tile
 
 
 def after(x, *done):
@@ -222,12 +251,13 @@
             out.append(int(slot[(p - way * step) % n_chips]))
         return out
 
-    own, other = contributions(g_occupied, g_virtual, owner, n_col)
+    column = tile_columns(n_col)
+    own, other = contributions(g_occupied, g_virtual, owner, column, n_col)
     mine = coulomb.T
     shard = mine.shape[0]
     first, second, swapped = {0: mine}, {}, {}
-    got = {"own": own}
-    out, tile = None, None
+    got = {"own": own, "column": column}
+    out, tile, ready, held = None, None, None, []
 
     def moved(x, name, way):
         with jax.named_scope(name):
@@ -267,13 +297,12 @@
                 else:
                     both, at = swapped[-i]
                     plan.append((places(i), (add(both), at + shard), (add(both), at)))
-            parts = 4 if half in steps else 1
             terms = [own, received] if tile is None else [tile]
-            result = columns(plan, parts, terms, pieces, shard, out, n_row * shard, COST.get(name, 1))
-            if tile is None:
-                result, tile = result
-            out = result
-            got[name] = tile if len(terms) == 2 else out
+            out, ready, tile = columns(
+                plan, terms, pieces, shard, ready, held, out, half in steps, n_row * shard, COST.get(name, 1)
+            )
+            held = [place for place, _, _ in plan]
+            got[name] = ready
     return out
 
 

time: 29.9 us -> 28.2 us (0.943)
  Pallas kernels: 8.55 us -> 5.83 us
  local copies, waits for them, and re-layouts: 0.09 us -> 0.7 us
    pallas_call x4 -> x5, Pallas kernels: 8.55 us -> 5.83 us  [the longest x3 4.37 us: columns(): pl.pallas_call(body, out_shape=out_shape, in_specs=in_specs, out_specs=ou...]
    unnamed x9 -> x10, local copies, waits for them, and re-layouts: 0.08 us -> 0.7 us
    ppermute x11 -> x12, starting transfers between devices: 14.6 us -> 14.7 us  [moved(): lax.ppermute(after(x, *(got[n] for n in AFTER.get(name, ()))), AXES, way)]
    ppermute x11 -> x12, waiting for transfers between devices: 6.45 us -> 6.51 us  [moved(): lax.ppermute(after(x, *(got[n] for n in AFTER.get(name, ()))), AXES, way)]
  transfers between devices with their start and end apart: 11 -> 12, of which waited for: 7 -> 6; matrix products, arithmetic and copies ran while one was open for 0% -> 0% of each run, Pallas kernels for 24% -> 15%
where the time goes in v3:
time: 28.2 us; the launch traced here: 28 us
  starting transfers between devices  14.7 us (52%)
  waiting for transfers between devices  6.51 us (23%)
  Pallas kernels  5.83 us (21%)
  local copies, waits for them, and re-layouts  0.7 us (2%)
    ppermute x12, starting transfers between devices, moved(): lax.ppermute(after(x, *(got[n] for n in AFTER.get(name, ()))), AXES, way)  14.7 us
    ppermute x12, waiting for transfers between devices, moved(): lax.ppermute(after(x, *(got[n] for n in AFTER.get(name, ()))), AXES, way)  6.51 us
    pallas_call x3, Pallas kernels, columns(): pl.pallas_call(body, out_shape=out_shape, in_specs=in_specs, out_specs=ou...  4.37 us
    pallas_call x1, Pallas kernels, contributions(): pl.pallas_call(contribution_kernel, out_shape=[jax.ShapeDtypeStruct((rows...  0.86 us
    unnamed x10, local copies, waits for them, and re-layouts  0.7 us
    pallas_call x1, Pallas kernels, tile_columns(): pl.pallas_call(functools.partial(tile_columns_kernel, n_col), out_shape=j...  0.6 us
  transfers between devices with their start and end apart: 12, of which 6 were waited for; matrix products, arithmetic and copies ran while one was open for 0% of the time, Pallas kernels for 15%

profile of v3, /device:TPU:0, one launch (start us, length us, event | category | flops | bytes accessed | tf_op | source)
XLA Modules:
  0.0 28.0 jit_solution(8717396310084621248)
XLA Ops:
  0.0 3.1 %collective-permute-start.2 = (bf16[192,512]{1,0:T(8,128)(2,1)}, bf16[192,512]{1,0:T(8,128)(2,1)S(1)}, u32[]{:S(2)}, u32[]{:S(2)}) collective-permute-start(bf16[192,512]{1,0:T(8,128)(2,1)} %bitcast.3), channel_id=1, source_target_pairs={{0,8},{1,9},{2,6},{3,7},{4,0},{5,1},{6,14},{7,15},{8,16},{9,17},{1... | collective-permute-start | bytes 589832 | tf_op jit(solution)/shard_map/first_1/ppermute | solution.py:264
  3.1 0.6 %tile_columns.1.column_ref = s32[8,128]{1,0:T(8,128)} custom-call(), custom_call_target="tpu_custom_call" | custom-call | flops 3221225472 | bytes 1024 | tf_op jit(solution)/shard_map/tile_columns/pallas_call | solution.py:85
  3.7 0.7 %copy-done.2 = s32[8,128]{1,0:T(8,128)S(1)} copy-done((s32[8,128]{1,0:T(8,128)S(1)}, s32[8,128]{1,0:T(8,128)}, u32[]{:S(2)}) %copy-start.2) | copy-done | bytes 4120
  4.4 0.9 %contributions.1 = (bf16[512,512]{1,0:T(8,128)(2,1)S(1)}, bf16[512,512]{1,0:T(8,128)(2,1)S(1)}) custom-call(s32[1,2]{1,0:T(1,128)S(1)} %bitcast.2, s32[8,128]{1,0:T(8,128)S(1)} %copy-done.2, bf16[2,512,512]{2,1,0:T(8,128)(2,1)S(1)} %copy-done, bf16[2,512,512]{2,1,0:T(8,128)(2,1)S(1)} %copy-done.1), custom_call_target="tpu_custom_call" | custom-call | flops 2097152 | bytes 2097152 | tf_op jit(solution)/shard_map/contributions/pallas_call | solution.py:110
  5.3 0.0 copy-start.4
  5.3 1.6 %collective-permute-start.3 = (bf16[192,512]{1,0:T(8,128)(2,1)S(1)}, bf16[192,512]{1,0:T(8,128)(2,1)S(1)}, u32[]{:S(2)}, u32[]{:S(2)}) collective-permute-start(bf16[192,512]{1,0:T(8,128)(2,1)S(1)} %collective-permute-done.1.refs_3_), channel_id=1, source_target_pairs={{0,8},{1,9},{2,6},{3,7},{4,0},{5,1},{6,14},{7,15},{8,16},{9,17},{1... | collective-permute-start | bytes 589832 | tf_op jit(solution)/shard_map/second_1/ppermute | solution.py:264
  6.9 2.1 %collective-permute-start.4 = (bf16[192,512]{1,0:T(8,128)(2,1)S(1)}, bf16[192,512]{1,0:T(8,128)(2,1)S(1)}, u32[]{:S(2)}, u32[]{:S(2)}) collective-permute-start(bf16[192,512]{1,0:T(8,128)(2,1)S(1)} %collective-permute-done.2.refs_4_), channel_id=1, source_target_pairs={{0,8},{1,9},{2,6},{3,7},{4,0},{5,1},{6,14},{7,15},{8,16},{9,17},{1... | collective-permute-start | bytes 589832 | tf_op jit(solution)/shard_map/first_2/ppermute | solution.py:264
  9.0 1.5 %collective-permute-start = (bf16[512,512]{1,0:T(8,128)(2,1)S(1)}, bf16[512,512]{1,0:T(8,128)(2,1)S(1)}, u32[]{:S(2)}, u32[]{:S(2)}) collective-permute-start(bf16[512,512]{1,0:T(8,128)(2,1)S(1)} %get-tuple-element.14), channel_id=1, source_target_pairs={{0,1},{1,0},{2,3},{3,2},{4,5},{5,4},{6,7},{7,6},{8,9},{9,8},{10,11... | collective-permute-start | bytes 1572872 | tf_op jit(solution)/shard_map/tile/ppermute | solution.py:264
  10.5 0.5 %collective-permute-done.3.refs_5_ = bf16[192,512]{1,0:T(8,128)(2,1)S(1)} collective-permute-done((bf16[192,512]{1,0:T(8,128)(2,1)S(1)}, bf16[192,512]{1,0:T(8,128)(2,1)S(1)}, u32[]{:S(2)}, u32[]{:S(2)}) %collective-permute-start.3) | collective-permute-done | bytes 196640 | tf_op jit(solution)/shard_map/second_1/ppermute | solution.py:264
  11.0 1.6 %collective-permute-start.8 = (bf16[192,512]{1,0:T(8,128)(2,1)S(1)}, bf16[192,512]{1,0:T(8,128)(2,1)S(1)}, u32[]{:S(2)}, u32[]{:S(2)}) collective-permute-start(bf16[192,512]{1,0:T(8,128)(2,1)S(1)} %collective-permute-done.3.refs_5_), channel_id=1, source_target_pairs={{0,8},{1,9},{2,6},{3,7},{4,0},{5,1},{6,14},{7,15},{8,16},{9,17},{1... | collective-permute-start | bytes 589832 | tf_op jit(solution)/shard_map/second_2/ppermute | solution.py:264
  12.6 0.5 %collective-permute-done.4.refs_1_ = bf16[192,512]{1,0:T(8,128)(2,1)S(1)} collective-permute-done((bf16[192,512]{1,0:T(8,128)(2,1)S(1)}, bf16[192,512]{1,0:T(8,128)(2,1)S(1)}, u32[]{:S(2)}, u32[]{:S(2)}) %collective-permute-start.4) | collective-permute-done | bytes 196640 | tf_op jit(solution)/shard_map/first_2/ppermute | solution.py:264
  13.1 1.6 %collective-permute-start.5 = (bf16[192,512]{1,0:T(8,128)(2,1)S(1)}, bf16[192,512]{1,0:T(8,128)(2,1)S(1)}, u32[]{:S(2)}, u32[]{:S(2)}) collective-permute-start(bf16[192,512]{1,0:T(8,128)(2,1)S(1)} %collective-permute-done.4.refs_1_), channel_id=1, source_target_pairs={{0,8},{1,9},{2,6},{3,7},{4,0},{5,1},{6,14},{7,15},{8,16},{9,17},{1... | collective-permute-start | bytes 589832 | tf_op jit(solution)/shard_map/first_3/ppermute | solution.py:264
  14.7 2.0 %collective-permute-done.8.refs_2_ = bf16[192,512]{1,0:T(8,128)(2,1)S(1)} collective-permute-done((bf16[192,512]{1,0:T(8,128)(2,1)S(1)}, bf16[192,512]{1,0:T(8,128)(2,1)S(1)}, u32[]{:S(2)}, u32[]{:S(2)}) %collective-permute-start.8) | collective-permute-done | bytes 196640 | tf_op jit(solution)/shard_map/second_2/ppermute | solution.py:264
  16.7 1.6 %collective-permute-start.9 = (bf16[192,512]{1,0:T(8,128)(2,1)S(1)}, bf16[192,512]{1,0:T(8,128)(2,1)S(1)}, u32[]{:S(2)}, u32[]{:S(2)}) collective-permute-start(bf16[192,512]{1,0:T(8,128)(2,1)S(1)} %collective-permute-done.8.refs_2_), channel_id=1, source_target_pairs={{0,8},{1,9},{2,6},{3,7},{4,0},{5,1},{6,14},{7,15},{8,16},{9,17},{1... | collective-permute-start | bytes 589832 | tf_op jit(solution)/shard_map/second_3/ppermute | solution.py:264
  18.2 0.5 %collective-permute-done.5.refs_3_ = bf16[192,512]{1,0:T(8,128)(2,1)S(1)} collective-permute-done((bf16[192,512]{1,0:T(8,128)(2,1)S(1)}, bf16[192,512]{1,0:T(8,128)(2,1)S(1)}, u32[]{:S(2)}, u32[]{:S(2)}) %collective-permute-start.5) | collective-permute-done | bytes 196640 | tf_op jit(solution)/shard_map/first_3/ppermute | solution.py:264
  18.8 1.6 %collective-permute-start.6 = (bf16[192,512]{1,0:T(8,128)(2,1)S(1)}, bf16[192,512]{1,0:T(8,128)(2,1)S(1)}, u32[]{:S(2)}, u32[]{:S(2)}) collective-permute-start(bf16[192,512]{1,0:T(8,128)(2,1)S(1)} %collective-permute-done.5.refs_3_), channel_id=1, source_target_pairs={{0,8},{1,9},{2,6},{3,7},{4,0},{5,1},{6,14},{7,15},{8,16},{9,17},{1... | collective-permute-start | bytes 589832 | tf_op jit(solution)/shard_map/first_4/ppermute | solution.py:264
  20.4 0.1 pad_maximum_fusion
  20.4 0.1 collective-permute-start.10
  20.5 1.9 %collective-permute-done.9.refs_4_ = bf16[192,512]{1,0:T(8,128)(2,1)S(1)} collective-permute-done((bf16[192,512]{1,0:T(8,128)(2,1)S(1)}, bf16[192,512]{1,0:T(8,128)(2,1)S(1)}, u32[]{:S(2)}, u32[]{:S(2)}) %collective-permute-start.9) | collective-permute-done | bytes 196640 | tf_op jit(solution)/shard_map/second_3/ppermute | solution.py:264
  22.4 0.1 collective-permute-start.11
  22.5 0.9 %columns.3 = (bf16[512,512]{1,0:T(8,128)(2,1)S(1)}, bf16[2,512,384]{2,1,0:T(8,128)(2,1)S(1)}) custom-call(bf16[512,512]{1,0:T(8,128)(2,1)S(1)} %get-tuple-element.13.refs_0_, bf16[512,512]{1,0:T(8,128)(2,1)S(1)} %collective-permute-done.refs_1_, bf16[192,512]{1,0:T(8,128)(2,1)S(1)} %bitcast.5, bf16[192,512]{1,0:T(8,128)(2,1)S(1)} %collective-permute-done.1.refs_3_, ...), custom_call_target="tpu_custom_call" | custom-call | flops 6442450944 | bytes 12582912 | tf_op jit(solution)/shard_map/columns/pallas_call | solution.py:201
  23.4 1.1 %collective-permute-done.6.refs_1_ = bf16[192,512]{1,0:T(8,128)(2,1)S(1)} collective-permute-done((bf16[192,512]{1,0:T(8,128)(2,1)S(1)}, bf16[192,512]{1,0:T(8,128)(2,1)S(1)}, u32[]{:S(2)}, u32[]{:S(2)}) %collective-permute-start.6) | collective-permute-done | bytes 196640 | tf_op jit(solution)/shard_map/first_4/ppermute | solution.py:264
  24.5 2.0 %columns.4 = (bf16[512,3072]{1,0:T(8,128)(2,1)}, bf16[5,512,384]{2,1,0:T(8,128)(2,1)S(1)}) custom-call(bf16[512,512]{1,0:T(8,128)(2,1)S(1)} %get-tuple-element.16.refs_0_, bf16[192,512]{1,0:T(8,128)(2,1)S(1)} %collective-permute-done.4.refs_1_, bf16[192,512]{1,0:T(8,128)(2,1)S(1)} %collective-permute-done.8.refs_2_, ...), custom_call_target="tpu_custom_call" | custom-call | flops 1006632960 | bytes 1966080 | tf_op jit(solution)/shard_map/columns/pallas_call | solution.py:201
  26.4 1.5 %columns.5 = bf16[512,3072]{1,0:T(8,128)(2,1)} custom-call(bf16[512,512]{1,0:T(8,128)(2,1)S(1)} %get-tuple-element.16.refs_0_, bf16[192,512]{1,0:T(8,128)(2,1)S(1)} %collective-permute-done.6.refs_1_, bf16[192,512]{1,0:T(8,128)(2,1)S(1)} %collective-permute-done.7.refs_2_, ...), custom_call_target="tpu_custom_call", output_to_operand_aliasing={{}: (4, {})} | custom-call | flops 201326592 | bytes 393216 | tf_op jit(solution)/shard_map/columns/pallas_call | solution.py:201
  (17 shorter events, 0.1 us)
Async XLA Ops:
  0.0 3.7 %copy-start = (bf16[2,512,512]{2,1,0:T(8,128)(2,1)S(1)}, bf16[2,512,512]{2,1,0:T(8,128)(2,1)}, u32[]{:S(2)}) copy-start(bf16[2,512,512]{2,1,0:T(8,128)(2,1)} %occ_ref.1) | copy-start | bytes 3145732
  0.0 3.7 %copy-start.1 = (bf16[2,512,512]{2,1,0:T(8,128)(2,1)S(1)}, bf16[2,512,512]{2,1,0:T(8,128)(2,1)}, u32[]{:S(2)}) copy-start(bf16[2,512,512]{2,1,0:T(8,128)(2,1)} %vir_ref.1) | copy-start | bytes 3145732
  0.0 3.7 %copy-start.3 = (s32[2,1]{0,1:T(1,128)S(1)}, s32[2,1]{0,1:T(1,128)}, u32[]{:S(2)}) copy-start(s32[2,1]{0,1:T(1,128)} %param.6) | copy-start | bytes 28
  0.0 6.9 %collective-permute-start.2 = (bf16[192,512]{1,0:T(8,128)(2,1)}, bf16[192,512]{1,0:T(8,128)(2,1)S(1)}, u32[]{:S(2)}, u32[]{:S(2)}) collective-permute-start(bf16[192,512]{1,0:T(8,128)(2,1)} %bitcast.3), channel_id=1, source_target_pairs={{0,8},{1,9},{2,6},{3,7},{4,0},{5,1},{6,14},{7,15},{8,16},{9,17},{1... | collective-permute-start | bytes 589832 | tf_op jit(solution)/shard_map/first_1/ppermute | solution.py:264
  3.1 2.2 %collective-permute-start.1 = (bf16[192,512]{1,0:T(8,128)(2,1)}, bf16[192,512]{1,0:T(8,128)(2,1)S(1)}, u32[]{:S(2)}, u32[]{:S(2)}) collective-permute-start(bf16[192,512]{1,0:T(8,128)(2,1)} %bitcast.4), channel_id=1, source_target_pairs={{0,2},{1,3},{2,0},{3,1},{4,6},{5,7},{6,4},{7,5},{8,10},{9,11},{10,... | collective-permute-start | bytes 589832 | tf_op jit(solution)/shard_map/swap_0/ppermute | solution.py:264
  3.7 0.7 %copy-start.2 = (s32[8,128]{1,0:T(8,128)S(1)}, s32[8,128]{1,0:T(8,128)}, u32[]{:S(2)}) copy-start(s32[8,128]{1,0:T(8,128)} %tile_columns.1.column_ref) | copy-start | bytes 12292
  5.3 17.2 %copy-start.4 = (bf16[512,192]{0,1:T(8,128)(2,1)S(1)}, bf16[512,192]{0,1:T(8,128)(2,1)}, u32[]{:S(2)}) copy-start(bf16[512,192]{0,1:T(8,128)(2,1)} %param.7) | copy-start | bytes 589828
  5.3 5.7 %collective-permute-start.3 = (bf16[192,512]{1,0:T(8,128)(2,1)S(1)}, bf16[192,512]{1,0:T(8,128)(2,1)S(1)}, u32[]{:S(2)}, u32[]{:S(2)}) collective-permute-start(bf16[192,512]{1,0:T(8,128)(2,1)S(1)} %collective-permute-done.1.refs_3_), channel_id=1, source_target_pairs={{0,8},{1,9},{2,6},{3,7},{4,0},{5,1},{6,14},{7,15},{8,16},{9,17},{1... | collective-permute-start | bytes 589832 | tf_op jit(solution)/shard_map/second_1/ppermute | solution.py:264
  6.9 6.2 %collective-permute-start.4 = (bf16[192,512]{1,0:T(8,128)(2,1)S(1)}, bf16[192,512]{1,0:T(8,128)(2,1)S(1)}, u32[]{:S(2)}, u32[]{:S(2)}) collective-permute-start(bf16[192,512]{1,0:T(8,128)(2,1)S(1)} %collective-permute-done.2.refs_4_), channel_id=1, source_target_pairs={{0,8},{1,9},{2,6},{3,7},{4,0},{5,1},{6,14},{7,15},{8,16},{9,17},{1... | collective-permute-start | bytes 589832 | tf_op jit(solution)/shard_map/first_2/ppermute | solution.py:264
  9.0 13.5 %collective-permute-start = (bf16[512,512]{1,0:T(8,128)(2,1)S(1)}, bf16[512,512]{1,0:T(8,128)(2,1)S(1)}, u32[]{:S(2)}, u32[]{:S(2)}) collective-permute-start(bf16[512,512]{1,0:T(8,128)(2,1)S(1)} %get-tuple-element.14), channel_id=1, source_target_pairs={{0,1},{1,0},{2,3},{3,2},{4,5},{5,4},{6,7},{7,6},{8,9},{9,8},{10,11... | collective-permute-start | bytes 1572872 | tf_op jit(solution)/shard_map/tile/ppermute | solution.py:264
  11.0 5.7 %collective-permute-start.8 = (bf16[192,512]{1,0:T(8,128)(2,1)S(1)}, bf16[192,512]{1,0:T(8,128)(2,1)S(1)}, u32[]{:S(2)}, u32[]{:S(2)}) collective-permute-start(bf16[192,512]{1,0:T(8,128)(2,1)S(1)} %collective-permute-done.3.refs_5_), channel_id=1, source_target_pairs={{0,8},{1,9},{2,6},{3,7},{4,0},{5,1},{6,14},{7,15},{8,16},{9,17},{1... | collective-permute-start | bytes 589832 | tf_op jit(solution)/shard_map/second_2/ppermute | solution.py:264
  13.1 5.7 %collective-permute-start.5 = (bf16[192,512]{1,0:T(8,128)(2,1)S(1)}, bf16[192,512]{1,0:T(8,128)(2,1)S(1)}, u32[]{:S(2)}, u32[]{:S(2)}) collective-permute-start(bf16[192,512]{1,0:T(8,128)(2,1)S(1)} %collective-permute-done.4.refs_1_), channel_id=1, source_target_pairs={{0,8},{1,9},{2,6},{3,7},{4,0},{5,1},{6,14},{7,15},{8,16},{9,17},{1... | collective-permute-start | bytes 589832 | tf_op jit(solution)/shard_map/first_3/ppermute | solution.py:264
  16.7 5.7 %collective-permute-start.9 = (bf16[192,512]{1,0:T(8,128)(2,1)S(1)}, bf16[192,512]{1,0:T(8,128)(2,1)S(1)}, u32[]{:S(2)}, u32[]{:S(2)}) collective-permute-start(bf16[192,512]{1,0:T(8,128)(2,1)S(1)} %collective-permute-done.8.refs_2_), channel_id=1, source_target_pairs={{0,8},{1,9},{2,6},{3,7},{4,0},{5,1},{6,14},{7,15},{8,16},{9,17},{1... | collective-permute-start | bytes 589832 | tf_op jit(solution)/shard_map/second_3/ppermute | solution.py:264
  18.8 5.7 %collective-permute-start.6 = (bf16[192,512]{1,0:T(8,128)(2,1)S(1)}, bf16[192,512]{1,0:T(8,128)(2,1)S(1)}, u32[]{:S(2)}, u32[]{:S(2)}) collective-permute-start(bf16[192,512]{1,0:T(8,128)(2,1)S(1)} %collective-permute-done.5.refs_3_), channel_id=1, source_target_pairs={{0,8},{1,9},{2,6},{3,7},{4,0},{5,1},{6,14},{7,15},{8,16},{9,17},{1... | collective-permute-start | bytes 589832 | tf_op jit(solution)/shard_map/first_4/ppermute | solution.py:264
  20.4 4.0 %collective-permute-start.10 = (bf16[768,512]{1,0:T(8,128)(2,1)S(1)}, bf16[768,512]{1,0:T(8,128)(2,1)S(1)}, u32[]{:S(2)}, u32[]{:S(2)}) collective-permute-start(bf16[768,512]{1,0:T(8,128)(2,1)S(1)} %pad_maximum_fusion), channel_id=1, source_target_pairs={{0,2},{1,3},{2,0},{3,1},{4,6},{5,7},{6,4},{7,5},{8,10},{9,11},{10,... | collective-permute-start | bytes 2359304 | tf_op jit(solution)/shard_map/swap_1_2/ppermute | solution.py:264
  22.4 2.1 %collective-permute-start.11 = (bf16[384,512]{1,0:T(8,128)(2,1)S(1)}, bf16[384,512]{1,0:T(8,128)(2,1)S(1)}, u32[]{:S(2)}, u32[]{:S(2)}) collective-permute-start(bf16[384,512]{1,0:T(8,128)(2,1)S(1)} %pad_maximum_fusion.1), channel_id=1, source_target_pairs={{0,2},{1,3},{2,0},{3,1},{4,6},{5,7},{6,4},{7,5},{8,10},{9,11},{10,... | collective-permute-start | bytes 1179656 | tf_op jit(solution)/shard_map/swap_3/ppermute | solution.py:264
  24.4 2.0 %collective-permute-start.7 = (bf16[192,512]{1,0:T(8,128)(2,1)S(1)}, bf16[192,512]{1,0:T(8,128)(2,1)S(1)}, u32[]{:S(2)}, u32[]{:S(2)}) collective-permute-start(bf16[192,512]{1,0:T(8,128)(2,1)S(1)} %collective-permute-done.6.refs_1_), channel_id=1, source_target_pairs={{0,2},{1,3},{2,0},{3,1},{4,6},{5,7},{6,4},{7,5},{8,10},{9,11},{10,... | collective-permute-start | bytes 589832 | tf_op jit(solution)/shard_map/swap_4/ppermute | solution.py:264

commit v4 on v3

--- a/solution.py
+++ b/solution.py
@@ -27,14 +27,15 @@
     "tile",
     "swap_1_2",
     "swap_3",
-    "chips_0_1",
+    "chips_0_1_2_3",
     "swap_4",
-    "chips_2_3_-1_-2_-3",
+    "chips_-1_-2_-3",
     "chips_4",
 )
-AFTER = {"swap_4": ("chips_0_1",), "second_1": ("own",)}
-COST = {"chips_0_1": 16}
+AFTER = {"swap_4": ("chips_0_1_2_3",), "second_1": ("own",)}
+COST = {"chips_0_1_2_3": 8}
 FRONT = 3221225472
+DIRECT = 2
 
 
 def chip_ring(mesh):
@@ -120,30 +121,31 @@
     )(owner.reshape(1, pairs), column, g_occupied, g_virtual)
 
 
-def columns_kernel(shape, n_terms, n_pieces, plan, held, last, *refs):
+def columns_kernel(shard, n_terms, n_pieces, plan, direct, held, last, *refs):
     device = lax.axis_index("row")
     core = lax.rem(device, 2)
-    shard = shape[0]
     width = 2 * shard
     refs = list(refs)
     terms = [refs.pop(0) for _ in range(n_terms)]
     pieces = [refs.pop(0) for _ in range(n_pieces)]
-    ready = refs.pop(0) if held else None
+    ready = [refs.pop(0) for _ in held]
     sem, panel = refs.pop(), refs.pop()
     block = refs.pop()
     tile = terms[0] if n_terms == 1 else refs.pop()
     out = refs.pop() if refs else None
-
-    def put(source, place, span, n):
+    copies = []
+
+    def put(source, place, span):
         slot = place[0]
         for r, s in enumerate(place):
             slot = jnp.where(device == r, s, slot)
         at = pl.ds(pl.multiple_of(slot * width, width), width)
-        return pltpu.make_async_copy(source.at[span], out.at[span, at], sem.at[n])
-
-    copies = [put(ready.at[j], place, pl.ds(0, tile.shape[0]), j) for j, place in enumerate(held)]
-    for c in copies:
-        c.start()
+        copies.append(pltpu.make_async_copy(source.at[span], out.at[span, at], sem.at[len(copies)]))
+        copies[-1].start()
+
+    for blocks, places in zip(ready, held, strict=True):
+        for j, place in places:
+            put(blocks.at[j], place, pl.ds(0, tile.shape[0]))
     if n_terms == 2:
         tile[...] = (terms[0][...].astype(jnp.float32) + terms[1][...].astype(jnp.float32)).astype(tile.dtype)
     parts = 4 if last else 1
@@ -157,31 +159,26 @@
             block[j, span] = lax.dot_general(
                 tile[span], pair, (((1,), (1,)), ((), ())), preferred_element_type=jnp.float32
             ).astype(block.dtype)
-            if last:
-                copies.append(put(block.at[j], place, span, len(copies)))
-                copies[-1].start()
+            if j < direct:
+                put(block.at[j], place, span)
     for c in copies:
         c.wait()
 
 
-def columns(plan, terms, pieces, shard, ready, held, out, last, out_width, cost):
+def columns(plan, terms, pieces, shard, direct, ready, held, out, last, out_width, cost):
     rows, depth = terms[0].shape
     width = 2 * shard
-    wide = jax.ShapeDtypeStruct((rows, out_width), jnp.bfloat16)
     blocks = (len(plan), rows, width)
-    args = [*terms, *pieces]
+    args = [*terms, *pieces, *ready]
     in_specs = [VMEM] * len(args)
-    if held:
-        args.append(ready)
-        in_specs.append(VMEM)
     aliases = {}
-    if out is not None:
+    if last and out is not None:
         aliases = {len(args): 0}
         args.append(out)
         in_specs.append(ANY)
     out_shape, out_specs = [], []
-    if held or last:
-        out_shape.append(wide)
+    if direct:
+        out_shape.append(jax.ShapeDtypeStruct((rows, out_width), jnp.bfloat16))
         out_specs.append(ANY)
     if len(terms) == 2:
         out_shape.append(jax.ShapeDtypeStruct((rows, depth), jnp.bfloat16))
@@ -189,24 +186,23 @@
     if not last:
         out_shape.append(jax.ShapeDtypeStruct(blocks, jnp.bfloat16))
         out_specs.append(VMEM)
-    scratch = [pltpu.VMEM(blocks, jnp.bfloat16)] if last else []
     n_in = len(args)
 
     def body(*refs):
         refs = list(refs)
-        if out is not None:
+        if aliases:
             del refs[n_in - 1]
-        columns_kernel((shard, width), len(terms), len(pieces), plan, held, last, *refs)
+        columns_kernel(shard, len(terms), len(pieces), plan, direct, held, last, *refs)
 
     result = pl.pallas_call(
         body,
         out_shape=out_shape,
         in_specs=in_specs,
         out_specs=out_specs,
-        scratch_shapes=scratch
+        scratch_shapes=([pltpu.VMEM(blocks, jnp.bfloat16)] if last else [])
         + [
             pltpu.VMEM((len(plan), 2, shard, depth), jnp.bfloat16),
-            pltpu.SemaphoreType.DMA((len(held) + 4 * len(plan),)),
+            pltpu.SemaphoreType.DMA((sum(len(h) for h in held) + 4 * len(plan),)),
         ],
         input_output_aliases=aliases,
         compiler_params=pltpu.CompilerParams(vmem_limit_bytes=16 << 20),
@@ -218,7 +214,7 @@
         name="columns",
     )(*args)
     result = list(result)
-    out = result.pop(0) if held or last else None
+    out = result.pop(0) if direct else out
     tile = result.pop(0) if len(terms) == 2 else terms[0]
     return out, None if last else result.pop(0), tile
 
@@ -257,7 +253,7 @@
     shard = mine.shape[0]
     first, second, swapped = {0: mine}, {}, {}
     got = {"own": own, "column": column}
-    out, tile, ready, held = None, None, None, []
+    out, tile, ready, held = None, None, [], []
 
     def moved(x, name, way):
         with jax.named_scope(name):
@@ -298,11 +294,15 @@
                     both, at = swapped[-i]
                     plan.append((places(i), (add(both), at + shard), (add(both), at)))
             terms = [own, received] if tile is None else [tile]
-            out, ready, tile = columns(
-                plan, terms, pieces, shard, ready, held, out, half in steps, n_row * shard, COST.get(name, 1)
+            last = half in steps
+            direct = len(plan) if last else DIRECT if tile is None else 0
+            out, blocks, tile = columns(
+                plan, terms, pieces, shard, direct, ready if last else [], held if last else [], out, last,
+                n_row * shard, COST.get(name, 1),
             )
-            held = [place for place, _, _ in plan]
-            got[name] = ready
+            ready.append(blocks)
+            held.append([(j, plan[j][0]) for j in range(direct, len(plan))])
+            got[name] = blocks
     return out
 
 

time: 28.2 us -> 27.6 us (0.979)
  waiting for transfers between devices: 6.51 us -> 5.67 us
  starting transfers between devices: 14.7 us -> 15 us
    ppermute x12, waiting for transfers between devices: 6.51 us -> 5.67 us  [moved(): lax.ppermute(after(x, *(got[n] for n in AFTER.get(name, ()))), AXES, way)]
    ppermute x12, starting transfers between devices: 14.7 us -> 15 us  [moved(): lax.ppermute(after(x, *(got[n] for n in AFTER.get(name, ()))), AXES, way)]
  transfers between devices with their start and end apart: 12 -> 12, of which waited for: 6 -> 6; matrix products, arithmetic and copies ran while one was open for 0% -> 0% of each run, Pallas kernels for 15% -> 16%
where the time goes in v4:
time: 27.6 us; the launch traced here: 27.4 us
  starting transfers between devices  15 us (54%)
  Pallas kernels  5.84 us (21%)
  waiting for transfers between devices  5.67 us (21%)
  local copies, waits for them, and re-layouts  0.7 us (3%)
    ppermute x12, starting transfers between devices, moved(): lax.ppermute(after(x, *(got[n] for n in AFTER.get(name, ()))), AXES, way)  15 us
    ppermute x12, waiting for transfers between devices, moved(): lax.ppermute(after(x, *(got[n] for n in AFTER.get(name, ()))), AXES, way)  5.67 us
    pallas_call x3, Pallas kernels, columns(): pl.pallas_call(body, out_shape=out_shape, in_specs=in_specs, out_specs=ou...  4.38 us
    pallas_call x1, Pallas kernels, contributions(): pl.pallas_call(contribution_kernel, out_shape=[jax.ShapeDtypeStruct((rows...  0.86 us
    unnamed x10, local copies, waits for them, and re-layouts  0.7 us
    pallas_call x1, Pallas kernels, tile_columns(): pl.pallas_call(functools.partial(tile_columns_kernel, n_col), out_shape=j...  0.6 us
  transfers between devices with their start and end apart: 12, of which 6 were waited for; matrix products, arithmetic and copies ran while one was open for 0% of the time, Pallas kernels for 16%

profile of v4, /device:TPU:0, one launch (start us, length us, event | category | flops | bytes accessed | tf_op | source)
XLA Modules:
  0.0 27.4 jit_solution(7263590050449785072)
XLA Ops:
  0.0 3.1 %collective-permute-start.2 = (bf16[192,512]{1,0:T(8,128)(2,1)}, bf16[192,512]{1,0:T(8,128)(2,1)S(1)}, u32[]{:S(2)}, u32[]{:S(2)}) collective-permute-start(bf16[192,512]{1,0:T(8,128)(2,1)} %bitcast.3), channel_id=1, source_target_pairs={{0,8},{1,9},{2,6},{3,7},{4,0},{5,1},{6,14},{7,15},{8,16},{9,17},{1... | collective-permute-start | bytes 589832 | tf_op jit(solution)/shard_map/first_1/ppermute | solution.py:260
  3.1 0.6 %tile_columns.1.column_ref = s32[8,128]{1,0:T(8,128)} custom-call(), custom_call_target="tpu_custom_call" | custom-call | flops 3221225472 | bytes 1024 | tf_op jit(solution)/shard_map/tile_columns/pallas_call | solution.py:86
  3.7 0.7 %copy-done.2 = s32[8,128]{1,0:T(8,128)S(1)} copy-done((s32[8,128]{1,0:T(8,128)S(1)}, s32[8,128]{1,0:T(8,128)}, u32[]{:S(2)}) %copy-start.2) | copy-done | bytes 4120
  4.4 0.9 %contributions.1 = (bf16[512,512]{1,0:T(8,128)(2,1)S(1)}, bf16[512,512]{1,0:T(8,128)(2,1)S(1)}) custom-call(s32[1,2]{1,0:T(1,128)S(1)} %bitcast.2, s32[8,128]{1,0:T(8,128)S(1)} %copy-done.2, bf16[2,512,512]{2,1,0:T(8,128)(2,1)S(1)} %copy-done, bf16[2,512,512]{2,1,0:T(8,128)(2,1)S(1)} %copy-done.1), custom_call_target="tpu_custom_call" | custom-call | flops 2097152 | bytes 2097152 | tf_op jit(solution)/shard_map/contributions/pallas_call | solution.py:111
  5.3 1.6 %collective-permute-start.3 = (bf16[192,512]{1,0:T(8,128)(2,1)S(1)}, bf16[192,512]{1,0:T(8,128)(2,1)S(1)}, u32[]{:S(2)}, u32[]{:S(2)}) collective-permute-start(bf16[192,512]{1,0:T(8,128)(2,1)S(1)} %collective-permute-done.1.refs_3_), channel_id=1, source_target_pairs={{0,8},{1,9},{2,6},{3,7},{4,0},{5,1},{6,14},{7,15},{8,16},{9,17},{1... | collective-permute-start | bytes 589832 | tf_op jit(solution)/shard_map/second_1/ppermute | solution.py:260
  6.9 2.1 %collective-permute-start.4 = (bf16[192,512]{1,0:T(8,128)(2,1)S(1)}, bf16[192,512]{1,0:T(8,128)(2,1)S(1)}, u32[]{:S(2)}, u32[]{:S(2)}) collective-permute-start(bf16[192,512]{1,0:T(8,128)(2,1)S(1)} %collective-permute-done.2.refs_4_), channel_id=1, source_target_pairs={{0,8},{1,9},{2,6},{3,7},{4,0},{5,1},{6,14},{7,15},{8,16},{9,17},{1... | collective-permute-start | bytes 589832 | tf_op jit(solution)/shard_map/first_2/ppermute | solution.py:260
  9.0 1.5 %collective-permute-start = (bf16[512,512]{1,0:T(8,128)(2,1)S(1)}, bf16[512,512]{1,0:T(8,128)(2,1)S(1)}, u32[]{:S(2)}, u32[]{:S(2)}) collective-permute-start(bf16[512,512]{1,0:T(8,128)(2,1)S(1)} %get-tuple-element.13), channel_id=1, source_target_pairs={{0,1},{1,0},{2,3},{3,2},{4,5},{5,4},{6,7},{7,6},{8,9},{9,8},{10,11... | collective-permute-start | bytes 1572872 | tf_op jit(solution)/shard_map/tile/ppermute | solution.py:260
  10.5 0.5 %collective-permute-done.3.refs_5_ = bf16[192,512]{1,0:T(8,128)(2,1)S(1)} collective-permute-done((bf16[192,512]{1,0:T(8,128)(2,1)S(1)}, bf16[192,512]{1,0:T(8,128)(2,1)S(1)}, u32[]{:S(2)}, u32[]{:S(2)}) %collective-permute-start.3) | collective-permute-done | bytes 196640 | tf_op jit(solution)/shard_map/second_1/ppermute | solution.py:260
  11.0 1.6 %collective-permute-start.5 = (bf16[192,512]{1,0:T(8,128)(2,1)S(1)}, bf16[192,512]{1,0:T(8,128)(2,1)S(1)}, u32[]{:S(2)}, u32[]{:S(2)}) collective-permute-start(bf16[192,512]{1,0:T(8,128)(2,1)S(1)} %collective-permute-done.3.refs_5_), channel_id=1, source_target_pairs={{0,8},{1,9},{2,6},{3,7},{4,0},{5,1},{6,14},{7,15},{8,16},{9,17},{1... | collective-permute-start | bytes 589832 | tf_op jit(solution)/shard_map/second_2/ppermute | solution.py:260
  12.6 0.5 %collective-permute-done.4.refs_6_ = bf16[192,512]{1,0:T(8,128)(2,1)S(1)} collective-permute-done((bf16[192,512]{1,0:T(8,128)(2,1)S(1)}, bf16[192,512]{1,0:T(8,128)(2,1)S(1)}, u32[]{:S(2)}, u32[]{:S(2)}) %collective-permute-start.4) | collective-permute-done | bytes 196640 | tf_op jit(solution)/shard_map/first_2/ppermute | solution.py:260
  13.1 1.6 %collective-permute-start.6 = (bf16[192,512]{1,0:T(8,128)(2,1)S(1)}, bf16[192,512]{1,0:T(8,128)(2,1)S(1)}, u32[]{:S(2)}, u32[]{:S(2)}) collective-permute-start(bf16[192,512]{1,0:T(8,128)(2,1)S(1)} %collective-permute-done.4.refs_6_), channel_id=1, source_target_pairs={{0,8},{1,9},{2,6},{3,7},{4,0},{5,1},{6,14},{7,15},{8,16},{9,17},{1... | collective-permute-start | bytes 589832 | tf_op jit(solution)/shard_map/first_3/ppermute | solution.py:260
  14.7 2.0 %collective-permute-done.5.refs_7_ = bf16[192,512]{1,0:T(8,128)(2,1)S(1)} collective-permute-done((bf16[192,512]{1,0:T(8,128)(2,1)S(1)}, bf16[192,512]{1,0:T(8,128)(2,1)S(1)}, u32[]{:S(2)}, u32[]{:S(2)}) %collective-permute-start.5) | collective-permute-done | bytes 196640 | tf_op jit(solution)/shard_map/second_2/ppermute | solution.py:260
  16.7 1.6 %collective-permute-start.7 = (bf16[192,512]{1,0:T(8,128)(2,1)S(1)}, bf16[192,512]{1,0:T(8,128)(2,1)S(1)}, u32[]{:S(2)}, u32[]{:S(2)}) collective-permute-start(bf16[192,512]{1,0:T(8,128)(2,1)S(1)} %collective-permute-done.5.refs_7_), channel_id=1, source_target_pairs={{0,8},{1,9},{2,6},{3,7},{4,0},{5,1},{6,14},{7,15},{8,16},{9,17},{1... | collective-permute-start | bytes 589832 | tf_op jit(solution)/shard_map/second_3/ppermute | solution.py:260
  18.2 0.5 %collective-permute-done.6.refs_8_ = bf16[192,512]{1,0:T(8,128)(2,1)S(1)} collective-permute-done((bf16[192,512]{1,0:T(8,128)(2,1)S(1)}, bf16[192,512]{1,0:T(8,128)(2,1)S(1)}, u32[]{:S(2)}, u32[]{:S(2)}) %collective-permute-start.6) | collective-permute-done | bytes 196640 | tf_op jit(solution)/shard_map/first_3/ppermute | solution.py:260
  18.8 1.6 %collective-permute-start.8 = (bf16[192,512]{1,0:T(8,128)(2,1)S(1)}, bf16[192,512]{1,0:T(8,128)(2,1)S(1)}, u32[]{:S(2)}, u32[]{:S(2)}) collective-permute-start(bf16[192,512]{1,0:T(8,128)(2,1)S(1)} %collective-permute-done.6.refs_8_), channel_id=1, source_target_pairs={{0,8},{1,9},{2,6},{3,7},{4,0},{5,1},{6,14},{7,15},{8,16},{9,17},{1... | collective-permute-start | bytes 589832 | tf_op jit(solution)/shard_map/first_4/ppermute | solution.py:260
  20.4 0.1 pad_maximum_fusion
  20.4 0.1 collective-permute-start.10
  20.5 1.9 %collective-permute-done.7.refs_9_ = bf16[192,512]{1,0:T(8,128)(2,1)S(1)} collective-permute-done((bf16[192,512]{1,0:T(8,128)(2,1)S(1)}, bf16[192,512]{1,0:T(8,128)(2,1)S(1)}, u32[]{:S(2)}, u32[]{:S(2)}) %collective-permute-start.7) | collective-permute-done | bytes 196640 | tf_op jit(solution)/shard_map/second_3/ppermute | solution.py:260
  22.4 0.1 collective-permute-start.11
  22.5 1.7 %columns.3 = (bf16[512,3072]{1,0:T(8,128)(2,1)}, bf16[512,512]{1,0:T(8,128)(2,1)S(1)}, bf16[4,512,384]{2,1,0:T(8,128)(2,1)S(1)}) custom-call(bf16[512,512]{1,0:T(8,128)(2,1)S(1)} %get-tuple-element.12.refs_0_, bf16[512,512]{1,0:T(8,128)(2,1)S(1)} %collective-permute-done.refs_1_, bf16[192,512]{1,0:T(8,128)(2,1)S(1)} %bitcast.5, ...), custom_call_target="tpu_custom_call" | custom-call | flops 6442450944 | bytes 12582912 | tf_op jit(solution)/shard_map/columns/pallas_call | solution.py:197
  24.2 0.3 collective-permute-done.8.refs_1_
  24.4 0.3 %collective-permute-start.9 = (bf16[192,512]{1,0:T(8,128)(2,1)S(1)}, bf16[192,512]{1,0:T(8,128)(2,1)S(1)}, u32[]{:S(2)}, u32[]{:S(2)}) collective-permute-start(bf16[192,512]{1,0:T(8,128)(2,1)S(1)} %collective-permute-done.8.refs_1_), channel_id=1, source_target_pairs={{0,2},{1,3},{2,0},{3,1},{4,6},{5,7},{6,4},{7,5},{8,10},{9,11},{10,... | collective-permute-start | bytes 589832 | tf_op jit(solution)/shard_map/swap_4/ppermute | solution.py:260
  24.8 1.2 %columns.4.refs_4_ = bf16[3,512,384]{2,1,0:T(8,128)(2,1)S(1)} custom-call(bf16[512,512]{1,0:T(8,128)(2,1)S(1)} %get-tuple-element.15.refs_0_, bf16[768,512]{1,0:T(8,128)(2,1)S(1)} %collective-permute-done.10.refs_1_, bf16[384,512]{1,0:T(8,128)(2,1)S(1)} %collective-permute-done.11.refs_2_), custom_call_target="tpu_custom_call" | custom-call | flops 603979776 | bytes 1179648 | tf_op jit(solution)/shard_map/columns/pallas_call | solution.py:197
  25.9 1.5 %columns.5 = bf16[512,3072]{1,0:T(8,128)(2,1)} custom-call(bf16[512,512]{1,0:T(8,128)(2,1)S(1)} %get-tuple-element.15.refs_0_, bf16[192,512]{1,0:T(8,128)(2,1)S(1)} %collective-permute-done.8.refs_1_, bf16[192,512]{1,0:T(8,128)(2,1)S(1)} %collective-permute-done.9.refs_2_, ...), custom_call_target="tpu_custom_call", output_to_operand_aliasing={{}: (5, {})} | custom-call | flops 201326592 | bytes 393216 | tf_op jit(solution)/shard_map/columns/pallas_call | solution.py:197
  (17 shorter events, 0.1 us)
Async XLA Ops:
  0.0 3.7 %copy-start = (bf16[2,512,512]{2,1,0:T(8,128)(2,1)S(1)}, bf16[2,512,512]{2,1,0:T(8,128)(2,1)}, u32[]{:S(2)}) copy-start(bf16[2,512,512]{2,1,0:T(8,128)(2,1)} %occ_ref.1) | copy-start | bytes 3145732
  0.0 3.7 %copy-start.1 = (bf16[2,512,512]{2,1,0:T(8,128)(2,1)S(1)}, bf16[2,512,512]{2,1,0:T(8,128)(2,1)}, u32[]{:S(2)}) copy-start(bf16[2,512,512]{2,1,0:T(8,128)(2,1)} %vir_ref.1) | copy-start | bytes 3145732
  0.0 3.7 %copy-start.3 = (s32[2,1]{0,1:T(1,128)S(1)}, s32[2,1]{0,1:T(1,128)}, u32[]{:S(2)}) copy-start(s32[2,1]{0,1:T(1,128)} %param.6) | copy-start | bytes 28
  0.0 6.9 %collective-permute-start.2 = (bf16[192,512]{1,0:T(8,128)(2,1)}, bf16[192,512]{1,0:T(8,128)(2,1)S(1)}, u32[]{:S(2)}, u32[]{:S(2)}) collective-permute-start(bf16[192,512]{1,0:T(8,128)(2,1)} %bitcast.3), channel_id=1, source_target_pairs={{0,8},{1,9},{2,6},{3,7},{4,0},{5,1},{6,14},{7,15},{8,16},{9,17},{1... | collective-permute-start | bytes 589832 | tf_op jit(solution)/shard_map/first_1/ppermute | solution.py:260
  3.1 2.2 %collective-permute-start.1 = (bf16[192,512]{1,0:T(8,128)(2,1)}, bf16[192,512]{1,0:T(8,128)(2,1)S(1)}, u32[]{:S(2)}, u32[]{:S(2)}) collective-permute-start(bf16[192,512]{1,0:T(8,128)(2,1)} %bitcast.4), channel_id=1, source_target_pairs={{0,2},{1,3},{2,0},{3,1},{4,6},{5,7},{6,4},{7,5},{8,10},{9,11},{10,... | collective-permute-start | bytes 589832 | tf_op jit(solution)/shard_map/swap_0/ppermute | solution.py:260
  3.7 0.7 %copy-start.2 = (s32[8,128]{1,0:T(8,128)S(1)}, s32[8,128]{1,0:T(8,128)}, u32[]{:S(2)}) copy-start(s32[8,128]{1,0:T(8,128)} %tile_columns.1.column_ref) | copy-start | bytes 12292
  5.3 17.2 %copy-start.4 = (bf16[512,192]{0,1:T(8,128)(2,1)S(1)}, bf16[512,192]{0,1:T(8,128)(2,1)}, u32[]{:S(2)}) copy-start(bf16[512,192]{0,1:T(8,128)(2,1)} %param.7) | copy-start | bytes 589828
  5.3 5.7 %collective-permute-start.3 = (bf16[192,512]{1,0:T(8,128)(2,1)S(1)}, bf16[192,512]{1,0:T(8,128)(2,1)S(1)}, u32[]{:S(2)}, u32[]{:S(2)}) collective-permute-start(bf16[192,512]{1,0:T(8,128)(2,1)S(1)} %collective-permute-done.1.refs_3_), channel_id=1, source_target_pairs={{0,8},{1,9},{2,6},{3,7},{4,0},{5,1},{6,14},{7,15},{8,16},{9,17},{1... | collective-permute-start | bytes 589832 | tf_op jit(solution)/shard_map/second_1/ppermute | solution.py:260
  6.9 6.2 %collective-permute-start.4 = (bf16[192,512]{1,0:T(8,128)(2,1)S(1)}, bf16[192,512]{1,0:T(8,128)(2,1)S(1)}, u32[]{:S(2)}, u32[]{:S(2)}) collective-permute-start(bf16[192,512]{1,0:T(8,128)(2,1)S(1)} %collective-permute-done.2.refs_4_), channel_id=1, source_target_pairs={{0,8},{1,9},{2,6},{3,7},{4,0},{5,1},{6,14},{7,15},{8,16},{9,17},{1... | collective-permute-start | bytes 589832 | tf_op jit(solution)/shard_map/first_2/ppermute | solution.py:260
  9.0 13.5 %collective-permute-start = (bf16[512,512]{1,0:T(8,128)(2,1)S(1)}, bf16[512,512]{1,0:T(8,128)(2,1)S(1)}, u32[]{:S(2)}, u32[]{:S(2)}) collective-permute-start(bf16[512,512]{1,0:T(8,128)(2,1)S(1)} %get-tuple-element.13), channel_id=1, source_target_pairs={{0,1},{1,0},{2,3},{3,2},{4,5},{5,4},{6,7},{7,6},{8,9},{9,8},{10,11... | collective-permute-start | bytes 1572872 | tf_op jit(solution)/shard_map/tile/ppermute | solution.py:260
  11.0 5.7 %collective-permute-start.5 = (bf16[192,512]{1,0:T(8,128)(2,1)S(1)}, bf16[192,512]{1,0:T(8,128)(2,1)S(1)}, u32[]{:S(2)}, u32[]{:S(2)}) collective-permute-start(bf16[192,512]{1,0:T(8,128)(2,1)S(1)} %collective-permute-done.3.refs_5_), channel_id=1, source_target_pairs={{0,8},{1,9},{2,6},{3,7},{4,0},{5,1},{6,14},{7,15},{8,16},{9,17},{1... | collective-permute-start | bytes 589832 | tf_op jit(solution)/shard_map/second_2/ppermute | solution.py:260
  13.1 5.7 %collective-permute-start.6 = (bf16[192,512]{1,0:T(8,128)(2,1)S(1)}, bf16[192,512]{1,0:T(8,128)(2,1)S(1)}, u32[]{:S(2)}, u32[]{:S(2)}) collective-permute-start(bf16[192,512]{1,0:T(8,128)(2,1)S(1)} %collective-permute-done.4.refs_6_), channel_id=1, source_target_pairs={{0,8},{1,9},{2,6},{3,7},{4,0},{5,1},{6,14},{7,15},{8,16},{9,17},{1... | collective-permute-start | bytes 589832 | tf_op jit(solution)/shard_map/first_3/ppermute | solution.py:260
  16.7 5.7 %collective-permute-start.7 = (bf16[192,512]{1,0:T(8,128)(2,1)S(1)}, bf16[192,512]{1,0:T(8,128)(2,1)S(1)}, u32[]{:S(2)}, u32[]{:S(2)}) collective-permute-start(bf16[192,512]{1,0:T(8,128)(2,1)S(1)} %collective-permute-done.5.refs_7_), channel_id=1, source_target_pairs={{0,8},{1,9},{2,6},{3,7},{4,0},{5,1},{6,14},{7,15},{8,16},{9,17},{1... | collective-permute-start | bytes 589832 | tf_op jit(solution)/shard_map/second_3/ppermute | solution.py:260
  18.8 5.7 %collective-permute-start.8 = (bf16[192,512]{1,0:T(8,128)(2,1)S(1)}, bf16[192,512]{1,0:T(8,128)(2,1)S(1)}, u32[]{:S(2)}, u32[]{:S(2)}) collective-permute-start(bf16[192,512]{1,0:T(8,128)(2,1)S(1)} %collective-permute-done.6.refs_8_), channel_id=1, source_target_pairs={{0,8},{1,9},{2,6},{3,7},{4,0},{5,1},{6,14},{7,15},{8,16},{9,17},{1... | collective-permute-start | bytes 589832 | tf_op jit(solution)/shard_map/first_4/ppermute | solution.py:260
  20.4 4.3 %collective-permute-start.10 = (bf16[768,512]{1,0:T(8,128)(2,1)S(1)}, bf16[768,512]{1,0:T(8,128)(2,1)S(1)}, u32[]{:S(2)}, u32[]{:S(2)}) collective-permute-start(bf16[768,512]{1,0:T(8,128)(2,1)S(1)} %pad_maximum_fusion), channel_id=1, source_target_pairs={{0,2},{1,3},{2,0},{3,1},{4,6},{5,7},{6,4},{7,5},{8,10},{9,11},{10,... | collective-permute-start | bytes 2359304 | tf_op jit(solution)/shard_map/swap_1_2/ppermute | solution.py:260
  22.4 2.4 %collective-permute-start.11 = (bf16[384,512]{1,0:T(8,128)(2,1)S(1)}, bf16[384,512]{1,0:T(8,128)(2,1)S(1)}, u32[]{:S(2)}, u32[]{:S(2)}) collective-permute-start(bf16[384,512]{1,0:T(8,128)(2,1)S(1)} %pad_maximum_fusion.1), channel_id=1, source_target_pairs={{0,2},{1,3},{2,0},{3,1},{4,6},{5,7},{6,4},{7,5},{8,10},{9,11},{10,... | collective-permute-start | bytes 1179656 | tf_op jit(solution)/shard_map/swap_3/ppermute | solution.py:260
  24.4 1.5 %collective-permute-start.9 = (bf16[192,512]{1,0:T(8,128)(2,1)S(1)}, bf16[192,512]{1,0:T(8,128)(2,1)S(1)}, u32[]{:S(2)}, u32[]{:S(2)}) collective-permute-start(bf16[192,512]{1,0:T(8,128)(2,1)S(1)} %collective-permute-done.8.refs_1_), channel_id=1, source_target_pairs={{0,2},{1,3},{2,0},{3,1},{4,6},{5,7},{6,4},{7,5},{8,10},{9,11},{10,... | collective-permute-start | bytes 589832 | tf_op jit(solution)/shard_map/swap_4/ppermute | solution.py:260

commit v5 on v4

--- a/solution.py
+++ b/solution.py
@@ -32,7 +32,7 @@
     "chips_-1_-2_-3",
     "chips_4",
 )
-AFTER = {"swap_4": ("chips_0_1_2_3",), "second_1": ("own",)}
+AFTER = {"swap_4": ("chips_0_1_2_3",), "first_2": ("own",)}
 COST = {"chips_0_1_2_3": 8}
 FRONT = 3221225472
 DIRECT = 2

time: 27.6 us -> 27.2 us (0.986)
  waiting for transfers between devices: 5.67 us -> 4.25 us
  starting transfers between devices: 15 us -> 16.1 us
    ppermute x12, waiting for transfers between devices: 5.67 us -> 4.25 us  [moved(): lax.ppermute(after(x, *(got[n] for n in AFTER.get(name, ()))), AXES, way)]
    ppermute x12, starting transfers between devices: 15 us -> 16.1 us  [moved(): lax.ppermute(after(x, *(got[n] for n in AFTER.get(name, ()))), AXES, way)]
where the time goes in v5:
time: 27.2 us; the launch traced here: 27 us
  starting transfers between devices  16.1 us (59%)
  Pallas kernels  5.84 us (21%)
  waiting for transfers between devices  4.25 us (16%)
  local copies, waits for them, and re-layouts  0.7 us (3%)
    ppermute x12, starting transfers between devices, moved(): lax.ppermute(after(x, *(got[n] for n in AFTER.get(name, ()))), AXES, way)  16.1 us
    pallas_call x3, Pallas kernels, columns(): pl.pallas_call(body, out_shape=out_shape, in_specs=in_specs, out_specs=ou...  4.38 us
    ppermute x12, waiting for transfers between devices, moved(): lax.ppermute(after(x, *(got[n] for n in AFTER.get(name, ()))), AXES, way)  4.25 us
    pallas_call x1, Pallas kernels, contributions(): pl.pallas_call(contribution_kernel, out_shape=[jax.ShapeDtypeStruct((rows...  0.86 us
    unnamed x10, local copies, waits for them, and re-layouts  0.7 us
    pallas_call x1, Pallas kernels, tile_columns(): pl.pallas_call(functools.partial(tile_columns_kernel, n_col), out_shape=j...  0.6 us
  transfers between devices with their start and end apart: 12, of which 6 were waited for; matrix products, arithmetic and copies ran while one was open for 0% of the time, Pallas kernels for 16%

profile of v5, /device:TPU:0, one launch (start us, length us, event | category | flops | bytes accessed | tf_op | source)
XLA Modules:
  0.0 27.0 jit_solution(1994319716163330537)
XLA Ops:
  0.0 0.5 %collective-permute-start.1 = (bf16[192,512]{1,0:T(8,128)(2,1)}, bf16[192,512]{1,0:T(8,128)(2,1)S(1)}, u32[]{:S(2)}, u32[]{:S(2)}) collective-permute-start(bf16[192,512]{1,0:T(8,128)(2,1)} %bitcast.3), channel_id=1, source_target_pairs={{0,2},{1,3},{2,0},{3,1},{4,6},{5,7},{6,4},{7,5},{8,10},{9,11},{10,... | collective-permute-start | bytes 589832 | tf_op jit(solution)/shard_map/swap_0/ppermute | solution.py:260
  0.5 2.6 %collective-permute-start.2 = (bf16[192,512]{1,0:T(8,128)(2,1)}, bf16[192,512]{1,0:T(8,128)(2,1)S(1)}, u32[]{:S(2)}, u32[]{:S(2)}) collective-permute-start(bf16[192,512]{1,0:T(8,128)(2,1)} %bitcast.4), channel_id=1, source_target_pairs={{0,8},{1,9},{2,6},{3,7},{4,0},{5,1},{6,14},{7,15},{8,16},{9,17},{1... | collective-permute-start | bytes 589832 | tf_op jit(solution)/shard_map/first_1/ppermute | solution.py:260
  3.2 1.6 %collective-permute-start.3 = (bf16[192,512]{1,0:T(8,128)(2,1)S(1)}, bf16[192,512]{1,0:T(8,128)(2,1)S(1)}, u32[]{:S(2)}, u32[]{:S(2)}) collective-permute-start(bf16[192,512]{1,0:T(8,128)(2,1)S(1)} %collective-permute-done.1.refs_3_), channel_id=1, source_target_pairs={{0,8},{1,9},{2,6},{3,7},{4,0},{5,1},{6,14},{7,15},{8,16},{9,17},{1... | collective-permute-start | bytes 589832 | tf_op jit(solution)/shard_map/second_1/ppermute | solution.py:260
  4.8 0.6 %tile_columns.1.column_ref = s32[8,128]{1,0:T(8,128)} custom-call(), custom_call_target="tpu_custom_call" | custom-call | flops 3221225472 | bytes 1024 | tf_op jit(solution)/shard_map/tile_columns/pallas_call | solution.py:86
  5.4 0.7 %copy-done.2 = s32[8,128]{1,0:T(8,128)S(1)} copy-done((s32[8,128]{1,0:T(8,128)S(1)}, s32[8,128]{1,0:T(8,128)}, u32[]{:S(2)}) %copy-start.2) | copy-done | bytes 4120
  6.0 0.9 %contributions.1 = (bf16[512,512]{1,0:T(8,128)(2,1)S(1)}, bf16[512,512]{1,0:T(8,128)(2,1)S(1)}) custom-call(s32[1,2]{1,0:T(1,128)S(1)} %bitcast.2, s32[8,128]{1,0:T(8,128)S(1)} %copy-done.2, bf16[2,512,512]{2,1,0:T(8,128)(2,1)S(1)} %copy-done, bf16[2,512,512]{2,1,0:T(8,128)(2,1)S(1)} %copy-done.1), custom_call_target="tpu_custom_call" | custom-call | flops 2097152 | bytes 2097152 | tf_op jit(solution)/shard_map/contributions/pallas_call | solution.py:111
  6.9 2.1 %collective-permute-start.4 = (bf16[192,512]{1,0:T(8,128)(2,1)S(1)}, bf16[192,512]{1,0:T(8,128)(2,1)S(1)}, u32[]{:S(2)}, u32[]{:S(2)}) collective-permute-start(bf16[192,512]{1,0:T(8,128)(2,1)S(1)} %collective-permute-done.2.refs_4_), channel_id=1, source_target_pairs={{0,8},{1,9},{2,6},{3,7},{4,0},{5,1},{6,14},{7,15},{8,16},{9,17},{1... | collective-permute-start | bytes 589832 | tf_op jit(solution)/shard_map/first_2/ppermute | solution.py:260
  9.0 1.5 %collective-permute-start = (bf16[512,512]{1,0:T(8,128)(2,1)S(1)}, bf16[512,512]{1,0:T(8,128)(2,1)S(1)}, u32[]{:S(2)}, u32[]{:S(2)}) collective-permute-start(bf16[512,512]{1,0:T(8,128)(2,1)S(1)} %get-tuple-element.13), channel_id=1, source_target_pairs={{0,1},{1,0},{2,3},{3,2},{4,5},{5,4},{6,7},{7,6},{8,9},{9,8},{10,11... | collective-permute-start | bytes 1572872 | tf_op jit(solution)/shard_map/tile/ppermute | solution.py:260
  10.6 1.6 %collective-permute-start.5 = (bf16[192,512]{1,0:T(8,128)(2,1)S(1)}, bf16[192,512]{1,0:T(8,128)(2,1)S(1)}, u32[]{:S(2)}, u32[]{:S(2)}) collective-permute-start(bf16[192,512]{1,0:T(8,128)(2,1)S(1)} %collective-permute-done.3.refs_5_), channel_id=1, source_target_pairs={{0,8},{1,9},{2,6},{3,7},{4,0},{5,1},{6,14},{7,15},{8,16},{9,17},{1... | collective-permute-start | bytes 589832 | tf_op jit(solution)/shard_map/second_2/ppermute | solution.py:260
  12.1 0.5 %collective-permute-done.4.refs_6_ = bf16[192,512]{1,0:T(8,128)(2,1)S(1)} collective-permute-done((bf16[192,512]{1,0:T(8,128)(2,1)S(1)}, bf16[192,512]{1,0:T(8,128)(2,1)S(1)}, u32[]{:S(2)}, u32[]{:S(2)}) %collective-permute-start.4) | collective-permute-done | bytes 196640 | tf_op jit(solution)/shard_map/first_2/ppermute | solution.py:260
  12.7 2.1 %collective-permute-start.6 = (bf16[192,512]{1,0:T(8,128)(2,1)S(1)}, bf16[192,512]{1,0:T(8,128)(2,1)S(1)}, u32[]{:S(2)}, u32[]{:S(2)}) collective-permute-start(bf16[192,512]{1,0:T(8,128)(2,1)S(1)} %collective-permute-done.4.refs_6_), channel_id=1, source_target_pairs={{0,8},{1,9},{2,6},{3,7},{4,0},{5,1},{6,14},{7,15},{8,16},{9,17},{1... | collective-permute-start | bytes 589832 | tf_op jit(solution)/shard_map/first_3/ppermute | solution.py:260
  14.7 1.5 %collective-permute-done.5.refs_7_ = bf16[192,512]{1,0:T(8,128)(2,1)S(1)} collective-permute-done((bf16[192,512]{1,0:T(8,128)(2,1)S(1)}, bf16[192,512]{1,0:T(8,128)(2,1)S(1)}, u32[]{:S(2)}, u32[]{:S(2)}) %collective-permute-start.5) | collective-permute-done | bytes 196640 | tf_op jit(solution)/shard_map/second_2/ppermute | solution.py:260
  16.2 1.6 %collective-permute-start.7 = (bf16[192,512]{1,0:T(8,128)(2,1)S(1)}, bf16[192,512]{1,0:T(8,128)(2,1)S(1)}, u32[]{:S(2)}, u32[]{:S(2)}) collective-permute-start(bf16[192,512]{1,0:T(8,128)(2,1)S(1)} %collective-permute-done.5.refs_7_), channel_id=1, source_target_pairs={{0,8},{1,9},{2,6},{3,7},{4,0},{5,1},{6,14},{7,15},{8,16},{9,17},{1... | collective-permute-start | bytes 589832 | tf_op jit(solution)/shard_map/second_3/ppermute | solution.py:260
  17.8 0.5 %collective-permute-done.6.refs_8_ = bf16[192,512]{1,0:T(8,128)(2,1)S(1)} collective-permute-done((bf16[192,512]{1,0:T(8,128)(2,1)S(1)}, bf16[192,512]{1,0:T(8,128)(2,1)S(1)}, u32[]{:S(2)}, u32[]{:S(2)}) %collective-permute-start.6) | collective-permute-done | bytes 196640 | tf_op jit(solution)/shard_map/first_3/ppermute | solution.py:260
  18.3 2.0 %collective-permute-start.8 = (bf16[192,512]{1,0:T(8,128)(2,1)S(1)}, bf16[192,512]{1,0:T(8,128)(2,1)S(1)}, u32[]{:S(2)}, u32[]{:S(2)}) collective-permute-start(bf16[192,512]{1,0:T(8,128)(2,1)S(1)} %collective-permute-done.6.refs_8_), channel_id=1, source_target_pairs={{0,8},{1,9},{2,6},{3,7},{4,0},{5,1},{6,14},{7,15},{8,16},{9,17},{1... | collective-permute-start | bytes 589832 | tf_op jit(solution)/shard_map/first_4/ppermute | solution.py:260
  20.4 0.1 collective-permute-start.10
  20.5 1.4 %collective-permute-done.7.refs_9_ = bf16[192,512]{1,0:T(8,128)(2,1)S(1)} collective-permute-done((bf16[192,512]{1,0:T(8,128)(2,1)S(1)}, bf16[192,512]{1,0:T(8,128)(2,1)S(1)}, u32[]{:S(2)}, u32[]{:S(2)}) %collective-permute-start.7) | collective-permute-done | bytes 196640 | tf_op jit(solution)/shard_map/second_3/ppermute | solution.py:260
  21.9 0.1 collective-permute-start.11
  22.0 0.1 collective-permute-done.refs_1_
  22.1 1.7 %columns.3 = (bf16[512,3072]{1,0:T(8,128)(2,1)}, bf16[512,512]{1,0:T(8,128)(2,1)S(1)}, bf16[4,512,384]{2,1,0:T(8,128)(2,1)S(1)}) custom-call(bf16[512,512]{1,0:T(8,128)(2,1)S(1)} %get-tuple-element.12.refs_0_, bf16[512,512]{1,0:T(8,128)(2,1)S(1)} %collective-permute-done.refs_1_, bf16[192,512]{1,0:T(8,128)(2,1)S(1)} %bitcast.5, ...), custom_call_target="tpu_custom_call" | custom-call | flops 6442450944 | bytes 12582912 | tf_op jit(solution)/shard_map/columns/pallas_call | solution.py:197
  23.8 0.2 collective-permute-done.8.refs_1_
  24.0 0.3 %collective-permute-start.9 = (bf16[192,512]{1,0:T(8,128)(2,1)S(1)}, bf16[192,512]{1,0:T(8,128)(2,1)S(1)}, u32[]{:S(2)}, u32[]{:S(2)}) collective-permute-start(bf16[192,512]{1,0:T(8,128)(2,1)S(1)} %collective-permute-done.8.refs_1_), channel_id=1, source_target_pairs={{0,2},{1,3},{2,0},{3,1},{4,6},{5,7},{6,4},{7,5},{8,10},{9,11},{10,... | collective-permute-start | bytes 589832 | tf_op jit(solution)/shard_map/swap_4/ppermute | solution.py:260
  24.3 1.2 %columns.4.refs_4_ = bf16[3,512,384]{2,1,0:T(8,128)(2,1)S(1)} custom-call(bf16[512,512]{1,0:T(8,128)(2,1)S(1)} %get-tuple-element.15.refs_0_, bf16[768,512]{1,0:T(8,128)(2,1)S(1)} %collective-permute-done.10.refs_1_, bf16[384,512]{1,0:T(8,128)(2,1)S(1)} %collective-permute-done.11.refs_2_), custom_call_target="tpu_custom_call" | custom-call | flops 603979776 | bytes 1179648 | tf_op jit(solution)/shard_map/columns/pallas_call | solution.py:197
  25.5 1.5 %columns.5 = bf16[512,3072]{1,0:T(8,128)(2,1)} custom-call(bf16[512,512]{1,0:T(8,128)(2,1)S(1)} %get-tuple-element.15.refs_0_, bf16[192,512]{1,0:T(8,128)(2,1)S(1)} %collective-permute-done.8.refs_1_, bf16[192,512]{1,0:T(8,128)(2,1)S(1)} %collective-permute-done.9.refs_2_, ...), custom_call_target="tpu_custom_call", output_to_operand_aliasing={{}: (5, {})} | custom-call | flops 201326592 | bytes 393216 | tf_op jit(solution)/shard_map/columns/pallas_call | solution.py:197
  (17 shorter events, 0.1 us)
Async XLA Ops:
  0.0 5.4 %copy-start = (bf16[2,512,512]{2,1,0:T(8,128)(2,1)S(1)}, bf16[2,512,512]{2,1,0:T(8,128)(2,1)}, u32[]{:S(2)}) copy-start(bf16[2,512,512]{2,1,0:T(8,128)(2,1)} %occ_ref.1) | copy-start | bytes 3145732
  0.0 5.4 %copy-start.1 = (bf16[2,512,512]{2,1,0:T(8,128)(2,1)S(1)}, bf16[2,512,512]{2,1,0:T(8,128)(2,1)}, u32[]{:S(2)}) copy-start(bf16[2,512,512]{2,1,0:T(8,128)(2,1)} %vir_ref.1) | copy-start | bytes 3145732
  0.0 5.4 %copy-start.3 = (s32[2,1]{0,1:T(1,128)S(1)}, s32[2,1]{0,1:T(1,128)}, u32[]{:S(2)}) copy-start(s32[2,1]{0,1:T(1,128)} %param.6) | copy-start | bytes 28
  0.0 3.2 %collective-permute-start.1 = (bf16[192,512]{1,0:T(8,128)(2,1)}, bf16[192,512]{1,0:T(8,128)(2,1)S(1)}, u32[]{:S(2)}, u32[]{:S(2)}) collective-permute-start(bf16[192,512]{1,0:T(8,128)(2,1)} %bitcast.3), channel_id=1, source_target_pairs={{0,2},{1,3},{2,0},{3,1},{4,6},{5,7},{6,4},{7,5},{8,10},{9,11},{10,... | collective-permute-start | bytes 589832 | tf_op jit(solution)/shard_map/swap_0/ppermute | solution.py:260
  0.5 6.4 %collective-permute-start.2 = (bf16[192,512]{1,0:T(8,128)(2,1)}, bf16[192,512]{1,0:T(8,128)(2,1)S(1)}, u32[]{:S(2)}, u32[]{:S(2)}) collective-permute-start(bf16[192,512]{1,0:T(8,128)(2,1)} %bitcast.4), channel_id=1, source_target_pairs={{0,8},{1,9},{2,6},{3,7},{4,0},{5,1},{6,14},{7,15},{8,16},{9,17},{1... | collective-permute-start | bytes 589832 | tf_op jit(solution)/shard_map/first_1/ppermute | solution.py:260
  3.2 7.4 %collective-permute-start.3 = (bf16[192,512]{1,0:T(8,128)(2,1)S(1)}, bf16[192,512]{1,0:T(8,128)(2,1)S(1)}, u32[]{:S(2)}, u32[]{:S(2)}) collective-permute-start(bf16[192,512]{1,0:T(8,128)(2,1)S(1)} %collective-permute-done.1.refs_3_), channel_id=1, source_target_pairs={{0,8},{1,9},{2,6},{3,7},{4,0},{5,1},{6,14},{7,15},{8,16},{9,17},{1... | collective-permute-start | bytes 589832 | tf_op jit(solution)/shard_map/second_1/ppermute | solution.py:260
  5.4 0.7 %copy-start.2 = (s32[8,128]{1,0:T(8,128)S(1)}, s32[8,128]{1,0:T(8,128)}, u32[]{:S(2)}) copy-start(s32[8,128]{1,0:T(8,128)} %tile_columns.1.column_ref) | copy-start | bytes 12292
  6.9 15.2 %copy-start.4 = (bf16[512,192]{0,1:T(8,128)(2,1)S(1)}, bf16[512,192]{0,1:T(8,128)(2,1)}, u32[]{:S(2)}) copy-start(bf16[512,192]{0,1:T(8,128)(2,1)} %param.7) | copy-start | bytes 589828
  6.9 5.7 %collective-permute-start.4 = (bf16[192,512]{1,0:T(8,128)(2,1)S(1)}, bf16[192,512]{1,0:T(8,128)(2,1)S(1)}, u32[]{:S(2)}, u32[]{:S(2)}) collective-permute-start(bf16[192,512]{1,0:T(8,128)(2,1)S(1)} %collective-permute-done.2.refs_4_), channel_id=1, source_target_pairs={{0,8},{1,9},{2,6},{3,7},{4,0},{5,1},{6,14},{7,15},{8,16},{9,17},{1... | collective-permute-start | bytes 589832 | tf_op jit(solution)/shard_map/first_2/ppermute | solution.py:260
  9.0 13.1 %collective-permute-start = (bf16[512,512]{1,0:T(8,128)(2,1)S(1)}, bf16[512,512]{1,0:T(8,128)(2,1)S(1)}, u32[]{:S(2)}, u32[]{:S(2)}) collective-permute-start(bf16[512,512]{1,0:T(8,128)(2,1)S(1)} %get-tuple-element.13), channel_id=1, source_target_pairs={{0,1},{1,0},{2,3},{3,2},{4,5},{5,4},{6,7},{7,6},{8,9},{9,8},{10,11... | collective-permute-start | bytes 1572872 | tf_op jit(solution)/shard_map/tile/ppermute | solution.py:260
  10.6 5.7 %collective-permute-start.5 = (bf16[192,512]{1,0:T(8,128)(2,1)S(1)}, bf16[192,512]{1,0:T(8,128)(2,1)S(1)}, u32[]{:S(2)}, u32[]{:S(2)}) collective-permute-start(bf16[192,512]{1,0:T(8,128)(2,1)S(1)} %collective-permute-done.3.refs_5_), channel_id=1, source_target_pairs={{0,8},{1,9},{2,6},{3,7},{4,0},{5,1},{6,14},{7,15},{8,16},{9,17},{1... | collective-permute-start | bytes 589832 | tf_op jit(solution)/shard_map/second_2/ppermute | solution.py:260
  12.7 5.7 %collective-permute-start.6 = (bf16[192,512]{1,0:T(8,128)(2,1)S(1)}, bf16[192,512]{1,0:T(8,128)(2,1)S(1)}, u32[]{:S(2)}, u32[]{:S(2)}) collective-permute-start(bf16[192,512]{1,0:T(8,128)(2,1)S(1)} %collective-permute-done.4.refs_6_), channel_id=1, source_target_pairs={{0,8},{1,9},{2,6},{3,7},{4,0},{5,1},{6,14},{7,15},{8,16},{9,17},{1... | collective-permute-start | bytes 589832 | tf_op jit(solution)/shard_map/first_3/ppermute | solution.py:260
  16.2 5.7 %collective-permute-start.7 = (bf16[192,512]{1,0:T(8,128)(2,1)S(1)}, bf16[192,512]{1,0:T(8,128)(2,1)S(1)}, u32[]{:S(2)}, u32[]{:S(2)}) collective-permute-start(bf16[192,512]{1,0:T(8,128)(2,1)S(1)} %collective-permute-done.5.refs_7_), channel_id=1, source_target_pairs={{0,8},{1,9},{2,6},{3,7},{4,0},{5,1},{6,14},{7,15},{8,16},{9,17},{1... | collective-permute-start | bytes 589832 | tf_op jit(solution)/shard_map/second_3/ppermute | solution.py:260
  18.3 5.7 %collective-permute-start.8 = (bf16[192,512]{1,0:T(8,128)(2,1)S(1)}, bf16[192,512]{1,0:T(8,128)(2,1)S(1)}, u32[]{:S(2)}, u32[]{:S(2)}) collective-permute-start(bf16[192,512]{1,0:T(8,128)(2,1)S(1)} %collective-permute-done.6.refs_8_), channel_id=1, source_target_pairs={{0,8},{1,9},{2,6},{3,7},{4,0},{5,1},{6,14},{7,15},{8,16},{9,17},{1... | collective-permute-start | bytes 589832 | tf_op jit(solution)/shard_map/first_4/ppermute | solution.py:260
  20.4 3.9 %collective-permute-start.10 = (bf16[768,512]{1,0:T(8,128)(2,1)S(1)}, bf16[768,512]{1,0:T(8,128)(2,1)S(1)}, u32[]{:S(2)}, u32[]{:S(2)}) collective-permute-start(bf16[768,512]{1,0:T(8,128)(2,1)S(1)} %pad_maximum_fusion), channel_id=1, source_target_pairs={{0,2},{1,3},{2,0},{3,1},{4,6},{5,7},{6,4},{7,5},{8,10},{9,11},{10,... | collective-permute-start | bytes 2359304 | tf_op jit(solution)/shard_map/swap_1_2/ppermute | solution.py:260
  21.9 2.4 %collective-permute-start.11 = (bf16[384,512]{1,0:T(8,128)(2,1)S(1)}, bf16[384,512]{1,0:T(8,128)(2,1)S(1)}, u32[]{:S(2)}, u32[]{:S(2)}) collective-permute-start(bf16[384,512]{1,0:T(8,128)(2,1)S(1)} %pad_maximum_fusion.1), channel_id=1, source_target_pairs={{0,2},{1,3},{2,0},{3,1},{4,6},{5,7},{6,4},{7,5},{8,10},{9,11},{10,... | collective-permute-start | bytes 1179656 | tf_op jit(solution)/shard_map/swap_3/ppermute | solution.py:260
  24.0 1.5 %collective-permute-start.9 = (bf16[192,512]{1,0:T(8,128)(2,1)S(1)}, bf16[192,512]{1,0:T(8,128)(2,1)S(1)}, u32[]{:S(2)}, u32[]{:S(2)}) collective-permute-start(bf16[192,512]{1,0:T(8,128)(2,1)S(1)} %collective-permute-done.8.refs_1_), channel_id=1, source_target_pairs={{0,2},{1,3},{2,0},{3,1},{4,6},{5,7},{6,4},{7,5},{8,10},{9,11},{10,... | collective-permute-start | bytes 589832 | tf_op jit(solution)/shard_map/swap_4/ppermute | solution.py:260

commit v6 on v5

--- a/solution.py
+++ b/solution.py
@@ -150,17 +150,23 @@
         tile[...] = (terms[0][...].astype(jnp.float32) + terms[1][...].astype(jnp.float32)).astype(tile.dtype)
     parts = 4 if last else 1
     rows = tile.shape[0] // parts
-    for j, (place, here, there) in enumerate(plan):
-        panel[j, core] = pieces[here[0]][pl.ds(here[1], shard)]
-        panel[j, 1 - core] = pieces[there[0]][pl.ds(there[1], shard)]
-        pair = panel[j].reshape(width, panel.shape[3])
+    step = 1 if n_terms == 2 else 2
+    for j in range(0, len(plan), step):
+        chips = list(range(j, min(j + step, len(plan))))
+        for n in chips:
+            _, here, there = plan[n]
+            panel[n, core] = pieces[here[0]][pl.ds(here[1], shard)]
+            panel[n, 1 - core] = pieces[there[0]][pl.ds(there[1], shard)]
+        panels = panel[pl.ds(j, len(chips))].reshape(len(chips) * width, panel.shape[3])
         for i in range(parts):
             span = pl.ds(i * rows, rows)
-            block[j, span] = lax.dot_general(
-                tile[span], pair, (((1,), (1,)), ((), ())), preferred_element_type=jnp.float32
+            product = lax.dot_general(
+                tile[span], panels, (((1,), (1,)), ((), ())), preferred_element_type=jnp.float32
             ).astype(block.dtype)
-            if j < direct:
-                put(block.at[j], place, span)
+            for n in chips:
+                block[n, span] = product[:, (n - j) * width : (n - j + 1) * width]
+                if n < direct:
+                    put(block.at[n], plan[n][0], span)
     for c in copies:
         c.wait()
 

time: 27.2 us -> 27.1 us (level)
  transfers between devices with their start and end apart: 12 -> 12, of which waited for: 6 -> 7; matrix products, arithmetic and copies ran while one was open for 0% -> 0% of each run, Pallas kernels for 16% -> 16%
where the time goes in v6:
time: 27.1 us; the launch traced here: 27 us
  starting transfers between devices  16.1 us (59%)
  Pallas kernels  5.72 us (21%)
  waiting for transfers between devices  4.32 us (16%)
  local copies, waits for them, and re-layouts  0.7 us (3%)
    ppermute x12, starting transfers between devices, moved(): lax.ppermute(after(x, *(got[n] for n in AFTER.get(name, ()))), AXES, way)  16.1 us
    ppermute x12, waiting for transfers between devices, moved(): lax.ppermute(after(x, *(got[n] for n in AFTER.get(name, ()))), AXES, way)  4.32 us
    pallas_call x3, Pallas kernels, columns(): pl.pallas_call(body, out_shape=out_shape, in_specs=in_specs, out_specs=ou...  4.27 us
    pallas_call x1, Pallas kernels, contributions(): pl.pallas_call(contribution_kernel, out_shape=[jax.ShapeDtypeStruct((rows...  0.86 us
    unnamed x10, local copies, waits for them, and re-layouts  0.7 us
    pallas_call x1, Pallas kernels, tile_columns(): pl.pallas_call(functools.partial(tile_columns_kernel, n_col), out_shape=j...  0.6 us
  transfers between devices with their start and end apart: 12, of which 7 were waited for; matrix products, arithmetic and copies ran while one was open for 0% of the time, Pallas kernels for 16%

profile of v6, /device:TPU:0, one launch (start us, length us, event | category | flops | bytes accessed | tf_op | source)
XLA Modules:
  0.0 27.0 jit_solution(7991604779007504374)
XLA Ops:
  0.0 0.5 %collective-permute-start.1 = (bf16[192,512]{1,0:T(8,128)(2,1)}, bf16[192,512]{1,0:T(8,128)(2,1)S(1)}, u32[]{:S(2)}, u32[]{:S(2)}) collective-permute-start(bf16[192,512]{1,0:T(8,128)(2,1)} %bitcast.3), channel_id=1, source_target_pairs={{0,2},{1,3},{2,0},{3,1},{4,6},{5,7},{6,4},{7,5},{8,10},{9,11},{10,... | collective-permute-start | bytes 589832 | tf_op jit(solution)/shard_map/swap_0/ppermute | solution.py:266
  0.5 2.6 %collective-permute-start.2 = (bf16[192,512]{1,0:T(8,128)(2,1)}, bf16[192,512]{1,0:T(8,128)(2,1)S(1)}, u32[]{:S(2)}, u32[]{:S(2)}) collective-permute-start(bf16[192,512]{1,0:T(8,128)(2,1)} %bitcast.4), channel_id=1, source_target_pairs={{0,8},{1,9},{2,6},{3,7},{4,0},{5,1},{6,14},{7,15},{8,16},{9,17},{1... | collective-permute-start | bytes 589832 | tf_op jit(solution)/shard_map/first_1/ppermute | solution.py:266
  3.2 1.6 %collective-permute-start.3 = (bf16[192,512]{1,0:T(8,128)(2,1)S(1)}, bf16[192,512]{1,0:T(8,128)(2,1)S(1)}, u32[]{:S(2)}, u32[]{:S(2)}) collective-permute-start(bf16[192,512]{1,0:T(8,128)(2,1)S(1)} %collective-permute-done.1.refs_3_), channel_id=1, source_target_pairs={{0,8},{1,9},{2,6},{3,7},{4,0},{5,1},{6,14},{7,15},{8,16},{9,17},{1... | collective-permute-start | bytes 589832 | tf_op jit(solution)/shard_map/second_1/ppermute | solution.py:266
  4.8 0.6 %tile_columns.1.column_ref = s32[8,128]{1,0:T(8,128)} custom-call(), custom_call_target="tpu_custom_call" | custom-call | flops 3221225472 | bytes 1024 | tf_op jit(solution)/shard_map/tile_columns/pallas_call | solution.py:86
  5.4 0.7 %copy-done.2 = s32[8,128]{1,0:T(8,128)S(1)} copy-done((s32[8,128]{1,0:T(8,128)S(1)}, s32[8,128]{1,0:T(8,128)}, u32[]{:S(2)}) %copy-start.2) | copy-done | bytes 4120
  6.0 0.9 %contributions.1 = (bf16[512,512]{1,0:T(8,128)(2,1)S(1)}, bf16[512,512]{1,0:T(8,128)(2,1)S(1)}) custom-call(s32[1,2]{1,0:T(1,128)S(1)} %bitcast.2, s32[8,128]{1,0:T(8,128)S(1)} %copy-done.2, bf16[2,512,512]{2,1,0:T(8,128)(2,1)S(1)} %copy-done, bf16[2,512,512]{2,1,0:T(8,128)(2,1)S(1)} %copy-done.1), custom_call_target="tpu_custom_call" | custom-call | flops 2097152 | bytes 2097152 | tf_op jit(solution)/shard_map/contributions/pallas_call | solution.py:111
  6.9 2.1 %collective-permute-start.4 = (bf16[192,512]{1,0:T(8,128)(2,1)S(1)}, bf16[192,512]{1,0:T(8,128)(2,1)S(1)}, u32[]{:S(2)}, u32[]{:S(2)}) collective-permute-start(bf16[192,512]{1,0:T(8,128)(2,1)S(1)} %collective-permute-done.2.refs_4_), channel_id=1, source_target_pairs={{0,8},{1,9},{2,6},{3,7},{4,0},{5,1},{6,14},{7,15},{8,16},{9,17},{1... | collective-permute-start | bytes 589832 | tf_op jit(solution)/shard_map/first_2/ppermute | solution.py:266
  9.0 1.5 %collective-permute-start = (bf16[512,512]{1,0:T(8,128)(2,1)S(1)}, bf16[512,512]{1,0:T(8,128)(2,1)S(1)}, u32[]{:S(2)}, u32[]{:S(2)}) collective-permute-start(bf16[512,512]{1,0:T(8,128)(2,1)S(1)} %get-tuple-element.13), channel_id=1, source_target_pairs={{0,1},{1,0},{2,3},{3,2},{4,5},{5,4},{6,7},{7,6},{8,9},{9,8},{10,11... | collective-permute-start | bytes 1572872 | tf_op jit(solution)/shard_map/tile/ppermute | solution.py:266
  10.6 1.6 %collective-permute-start.5 = (bf16[192,512]{1,0:T(8,128)(2,1)S(1)}, bf16[192,512]{1,0:T(8,128)(2,1)S(1)}, u32[]{:S(2)}, u32[]{:S(2)}) collective-permute-start(bf16[192,512]{1,0:T(8,128)(2,1)S(1)} %collective-permute-done.3.refs_5_), channel_id=1, source_target_pairs={{0,8},{1,9},{2,6},{3,7},{4,0},{5,1},{6,14},{7,15},{8,16},{9,17},{1... | collective-permute-start | bytes 589832 | tf_op jit(solution)/shard_map/second_2/ppermute | solution.py:266
  12.1 0.5 %collective-permute-done.4.refs_6_ = bf16[192,512]{1,0:T(8,128)(2,1)S(1)} collective-permute-done((bf16[192,512]{1,0:T(8,128)(2,1)S(1)}, bf16[192,512]{1,0:T(8,128)(2,1)S(1)}, u32[]{:S(2)}, u32[]{:S(2)}) %collective-permute-start.4) | collective-permute-done | bytes 196640 | tf_op jit(solution)/shard_map/first_2/ppermute | solution.py:266
  12.7 2.1 %collective-permute-start.6 = (bf16[192,512]{1,0:T(8,128)(2,1)S(1)}, bf16[192,512]{1,0:T(8,128)(2,1)S(1)}, u32[]{:S(2)}, u32[]{:S(2)}) collective-permute-start(bf16[192,512]{1,0:T(8,128)(2,1)S(1)} %collective-permute-done.4.refs_6_), channel_id=1, source_target_pairs={{0,8},{1,9},{2,6},{3,7},{4,0},{5,1},{6,14},{7,15},{8,16},{9,17},{1... | collective-permute-start | bytes 589832 | tf_op jit(solution)/shard_map/first_3/ppermute | solution.py:266
  14.7 1.5 %collective-permute-done.5.refs_7_ = bf16[192,512]{1,0:T(8,128)(2,1)S(1)} collective-permute-done((bf16[192,512]{1,0:T(8,128)(2,1)S(1)}, bf16[192,512]{1,0:T(8,128)(2,1)S(1)}, u32[]{:S(2)}, u32[]{:S(2)}) %collective-permute-start.5) | collective-permute-done | bytes 196640 | tf_op jit(solution)/shard_map/second_2/ppermute | solution.py:266
  16.2 1.6 %collective-permute-start.7 = (bf16[192,512]{1,0:T(8,128)(2,1)S(1)}, bf16[192,512]{1,0:T(8,128)(2,1)S(1)}, u32[]{:S(2)}, u32[]{:S(2)}) collective-permute-start(bf16[192,512]{1,0:T(8,128)(2,1)S(1)} %collective-permute-done.5.refs_7_), channel_id=1, source_target_pairs={{0,8},{1,9},{2,6},{3,7},{4,0},{5,1},{6,14},{7,15},{8,16},{9,17},{1... | collective-permute-start | bytes 589832 | tf_op jit(solution)/shard_map/second_3/ppermute | solution.py:266
  17.8 0.5 %collective-permute-done.6.refs_8_ = bf16[192,512]{1,0:T(8,128)(2,1)S(1)} collective-permute-done((bf16[192,512]{1,0:T(8,128)(2,1)S(1)}, bf16[192,512]{1,0:T(8,128)(2,1)S(1)}, u32[]{:S(2)}, u32[]{:S(2)}) %collective-permute-start.6) | collective-permute-done | bytes 196640 | tf_op jit(solution)/shard_map/first_3/ppermute | solution.py:266
  18.3 2.0 %collective-permute-start.8 = (bf16[192,512]{1,0:T(8,128)(2,1)S(1)}, bf16[192,512]{1,0:T(8,128)(2,1)S(1)}, u32[]{:S(2)}, u32[]{:S(2)}) collective-permute-start(bf16[192,512]{1,0:T(8,128)(2,1)S(1)} %collective-permute-done.6.refs_8_), channel_id=1, source_target_pairs={{0,8},{1,9},{2,6},{3,7},{4,0},{5,1},{6,14},{7,15},{8,16},{9,17},{1... | collective-permute-start | bytes 589832 | tf_op jit(solution)/shard_map/first_4/ppermute | solution.py:266
  20.4 0.1 collective-permute-start.10
  20.5 1.4 %collective-permute-done.7.refs_9_ = bf16[192,512]{1,0:T(8,128)(2,1)S(1)} collective-permute-done((bf16[192,512]{1,0:T(8,128)(2,1)S(1)}, bf16[192,512]{1,0:T(8,128)(2,1)S(1)}, u32[]{:S(2)}, u32[]{:S(2)}) %collective-permute-start.7) | collective-permute-done | bytes 196640 | tf_op jit(solution)/shard_map/second_3/ppermute | solution.py:266
  21.9 0.1 collective-permute-start.11
  22.0 0.1 collective-permute-done.refs_1_
  22.1 1.7 %columns.3 = (bf16[512,3072]{1,0:T(8,128)(2,1)}, bf16[512,512]{1,0:T(8,128)(2,1)S(1)}, bf16[4,512,384]{2,1,0:T(8,128)(2,1)S(1)}) custom-call(bf16[512,512]{1,0:T(8,128)(2,1)S(1)} %get-tuple-element.12.refs_0_, bf16[512,512]{1,0:T(8,128)(2,1)S(1)} %collective-permute-done.refs_1_, bf16[192,512]{1,0:T(8,128)(2,1)S(1)} %bitcast.5, ...), custom_call_target="tpu_custom_call" | custom-call | flops 6442450944 | bytes 12582912 | tf_op jit(solution)/shard_map/columns/pallas_call | solution.py:203
  23.8 0.2 collective-permute-done.8.refs_1_
  24.0 0.3 %collective-permute-start.9 = (bf16[192,512]{1,0:T(8,128)(2,1)S(1)}, bf16[192,512]{1,0:T(8,128)(2,1)S(1)}, u32[]{:S(2)}, u32[]{:S(2)}) collective-permute-start(bf16[192,512]{1,0:T(8,128)(2,1)S(1)} %collective-permute-done.8.refs_1_), channel_id=1, source_target_pairs={{0,2},{1,3},{2,0},{3,1},{4,6},{5,7},{6,4},{7,5},{8,10},{9,11},{10,... | collective-permute-start | bytes 589832 | tf_op jit(solution)/shard_map/swap_4/ppermute | solution.py:266
  24.3 1.1 %columns.4.refs_4_ = bf16[3,512,384]{2,1,0:T(8,128)(2,1)S(1)} custom-call(bf16[512,512]{1,0:T(8,128)(2,1)S(1)} %get-tuple-element.15.refs_0_, bf16[768,512]{1,0:T(8,128)(2,1)S(1)} %collective-permute-done.10.refs_1_, bf16[384,512]{1,0:T(8,128)(2,1)S(1)} %collective-permute-done.11.refs_2_), custom_call_target="tpu_custom_call" | custom-call | flops 603979776 | bytes 1179648 | tf_op jit(solution)/shard_map/columns/pallas_call | solution.py:203
  25.5 1.5 %columns.5 = bf16[512,3072]{1,0:T(8,128)(2,1)} custom-call(bf16[512,512]{1,0:T(8,128)(2,1)S(1)} %get-tuple-element.15.refs_0_, bf16[192,512]{1,0:T(8,128)(2,1)S(1)} %collective-permute-done.8.refs_1_, bf16[192,512]{1,0:T(8,128)(2,1)S(1)} %collective-permute-done.9.refs_2_, ...), custom_call_target="tpu_custom_call", output_to_operand_aliasing={{}: (5, {})} | custom-call | flops 201326592 | bytes 393216 | tf_op jit(solution)/shard_map/columns/pallas_call | solution.py:203
  (17 shorter events, 0.2 us)
Async XLA Ops:
  0.0 5.4 %copy-start = (bf16[2,512,512]{2,1,0:T(8,128)(2,1)S(1)}, bf16[2,512,512]{2,1,0:T(8,128)(2,1)}, u32[]{:S(2)}) copy-start(bf16[2,512,512]{2,1,0:T(8,128)(2,1)} %occ_ref.1) | copy-start | bytes 3145732
  0.0 5.4 %copy-start.1 = (bf16[2,512,512]{2,1,0:T(8,128)(2,1)S(1)}, bf16[2,512,512]{2,1,0:T(8,128)(2,1)}, u32[]{:S(2)}) copy-start(bf16[2,512,512]{2,1,0:T(8,128)(2,1)} %vir_ref.1) | copy-start | bytes 3145732
  0.0 5.4 %copy-start.3 = (s32[2,1]{0,1:T(1,128)S(1)}, s32[2,1]{0,1:T(1,128)}, u32[]{:S(2)}) copy-start(s32[2,1]{0,1:T(1,128)} %param.6) | copy-start | bytes 28
  0.0 3.2 %collective-permute-start.1 = (bf16[192,512]{1,0:T(8,128)(2,1)}, bf16[192,512]{1,0:T(8,128)(2,1)S(1)}, u32[]{:S(2)}, u32[]{:S(2)}) collective-permute-start(bf16[192,512]{1,0:T(8,128)(2,1)} %bitcast.3), channel_id=1, source_target_pairs={{0,2},{1,3},{2,0},{3,1},{4,6},{5,7},{6,4},{7,5},{8,10},{9,11},{10,... | collective-permute-start | bytes 589832 | tf_op jit(solution)/shard_map/swap_0/ppermute | solution.py:266
  0.5 6.4 %collective-permute-start.2 = (bf16[192,512]{1,0:T(8,128)(2,1)}, bf16[192,512]{1,0:T(8,128)(2,1)S(1)}, u32[]{:S(2)}, u32[]{:S(2)}) collective-permute-start(bf16[192,512]{1,0:T(8,128)(2,1)} %bitcast.4), channel_id=1, source_target_pairs={{0,8},{1,9},{2,6},{3,7},{4,0},{5,1},{6,14},{7,15},{8,16},{9,17},{1... | collective-permute-start | bytes 589832 | tf_op jit(solution)/shard_map/first_1/ppermute | solution.py:266
  3.2 7.4 %collective-permute-start.3 = (bf16[192,512]{1,0:T(8,128)(2,1)S(1)}, bf16[192,512]{1,0:T(8,128)(2,1)S(1)}, u32[]{:S(2)}, u32[]{:S(2)}) collective-permute-start(bf16[192,512]{1,0:T(8,128)(2,1)S(1)} %collective-permute-done.1.refs_3_), channel_id=1, source_target_pairs={{0,8},{1,9},{2,6},{3,7},{4,0},{5,1},{6,14},{7,15},{8,16},{9,17},{1... | collective-permute-start | bytes 589832 | tf_op jit(solution)/shard_map/second_1/ppermute | solution.py:266
  5.4 0.7 %copy-start.2 = (s32[8,128]{1,0:T(8,128)S(1)}, s32[8,128]{1,0:T(8,128)}, u32[]{:S(2)}) copy-start(s32[8,128]{1,0:T(8,128)} %tile_columns.1.column_ref) | copy-start | bytes 12292
  6.9 15.2 %copy-start.4 = (bf16[512,192]{0,1:T(8,128)(2,1)S(1)}, bf16[512,192]{0,1:T(8,128)(2,1)}, u32[]{:S(2)}) copy-start(bf16[512,192]{0,1:T(8,128)(2,1)} %param.7) | copy-start | bytes 589828
  6.9 5.7 %collective-permute-start.4 = (bf16[192,512]{1,0:T(8,128)(2,1)S(1)}, bf16[192,512]{1,0:T(8,128)(2,1)S(1)}, u32[]{:S(2)}, u32[]{:S(2)}) collective-permute-start(bf16[192,512]{1,0:T(8,128)(2,1)S(1)} %collective-permute-done.2.refs_4_), channel_id=1, source_target_pairs={{0,8},{1,9},{2,6},{3,7},{4,0},{5,1},{6,14},{7,15},{8,16},{9,17},{1... | collective-permute-start | bytes 589832 | tf_op jit(solution)/shard_map/first_2/ppermute | solution.py:266
  9.0 13.1 %collective-permute-start = (bf16[512,512]{1,0:T(8,128)(2,1)S(1)}, bf16[512,512]{1,0:T(8,128)(2,1)S(1)}, u32[]{:S(2)}, u32[]{:S(2)}) collective-permute-start(bf16[512,512]{1,0:T(8,128)(2,1)S(1)} %get-tuple-element.13), channel_id=1, source_target_pairs={{0,1},{1,0},{2,3},{3,2},{4,5},{5,4},{6,7},{7,6},{8,9},{9,8},{10,11... | collective-permute-start | bytes 1572872 | tf_op jit(solution)/shard_map/tile/ppermute | solution.py:266
  10.6 5.7 %collective-permute-start.5 = (bf16[192,512]{1,0:T(8,128)(2,1)S(1)}, bf16[192,512]{1,0:T(8,128)(2,1)S(1)}, u32[]{:S(2)}, u32[]{:S(2)}) collective-permute-start(bf16[192,512]{1,0:T(8,128)(2,1)S(1)} %collective-permute-done.3.refs_5_), channel_id=1, source_target_pairs={{0,8},{1,9},{2,6},{3,7},{4,0},{5,1},{6,14},{7,15},{8,16},{9,17},{1... | collective-permute-start | bytes 589832 | tf_op jit(solution)/shard_map/second_2/ppermute | solution.py:266
  12.7 5.7 %collective-permute-start.6 = (bf16[192,512]{1,0:T(8,128)(2,1)S(1)}, bf16[192,512]{1,0:T(8,128)(2,1)S(1)}, u32[]{:S(2)}, u32[]{:S(2)}) collective-permute-start(bf16[192,512]{1,0:T(8,128)(2,1)S(1)} %collective-permute-done.4.refs_6_), channel_id=1, source_target_pairs={{0,8},{1,9},{2,6},{3,7},{4,0},{5,1},{6,14},{7,15},{8,16},{9,17},{1... | collective-permute-start | bytes 589832 | tf_op jit(solution)/shard_map/first_3/ppermute | solution.py:266
  16.2 5.7 %collective-permute-start.7 = (bf16[192,512]{1,0:T(8,128)(2,1)S(1)}, bf16[192,512]{1,0:T(8,128)(2,1)S(1)}, u32[]{:S(2)}, u32[]{:S(2)}) collective-permute-start(bf16[192,512]{1,0:T(8,128)(2,1)S(1)} %collective-permute-done.5.refs_7_), channel_id=1, source_target_pairs={{0,8},{1,9},{2,6},{3,7},{4,0},{5,1},{6,14},{7,15},{8,16},{9,17},{1... | collective-permute-start | bytes 589832 | tf_op jit(solution)/shard_map/second_3/ppermute | solution.py:266
  18.3 5.7 %collective-permute-start.8 = (bf16[192,512]{1,0:T(8,128)(2,1)S(1)}, bf16[192,512]{1,0:T(8,128)(2,1)S(1)}, u32[]{:S(2)}, u32[]{:S(2)}) collective-permute-start(bf16[192,512]{1,0:T(8,128)(2,1)S(1)} %collective-permute-done.6.refs_8_), channel_id=1, source_target_pairs={{0,8},{1,9},{2,6},{3,7},{4,0},{5,1},{6,14},{7,15},{8,16},{9,17},{1... | collective-permute-start | bytes 589832 | tf_op jit(solution)/shard_map/first_4/ppermute | solution.py:266
  20.4 3.9 %collective-permute-start.10 = (bf16[768,512]{1,0:T(8,128)(2,1)S(1)}, bf16[768,512]{1,0:T(8,128)(2,1)S(1)}, u32[]{:S(2)}, u32[]{:S(2)}) collective-permute-start(bf16[768,512]{1,0:T(8,128)(2,1)S(1)} %pad_maximum_fusion), channel_id=1, source_target_pairs={{0,2},{1,3},{2,0},{3,1},{4,6},{5,7},{6,4},{7,5},{8,10},{9,11},{10,... | collective-permute-start | bytes 2359304 | tf_op jit(solution)/shard_map/swap_1_2/ppermute | solution.py:266
  21.9 2.4 %collective-permute-start.11 = (bf16[384,512]{1,0:T(8,128)(2,1)S(1)}, bf16[384,512]{1,0:T(8,128)(2,1)S(1)}, u32[]{:S(2)}, u32[]{:S(2)}) collective-permute-start(bf16[384,512]{1,0:T(8,128)(2,1)S(1)} %pad_maximum_fusion.1), channel_id=1, source_target_pairs={{0,2},{1,3},{2,0},{3,1},{4,6},{5,7},{6,4},{7,5},{8,10},{9,11},{10,... | collective-permute-start | bytes 1179656 | tf_op jit(solution)/shard_map/swap_3/ppermute | solution.py:266
  24.0 1.4 %collective-permute-start.9 = (bf16[192,512]{1,0:T(8,128)(2,1)S(1)}, bf16[192,512]{1,0:T(8,128)(2,1)S(1)}, u32[]{:S(2)}, u32[]{:S(2)}) collective-permute-start(bf16[192,512]{1,0:T(8,128)(2,1)S(1)} %collective-permute-done.8.refs_1_), channel_id=1, source_target_pairs={{0,2},{1,3},{2,0},{3,1},{4,6},{5,7},{6,4},{7,5},{8,10},{9,11},{10,... | collective-permute-start | bytes 589832 | tf_op jit(solution)/shard_map/swap_4/ppermute | solution.py:266
